TPU v7x, 128 devices: a whole 4x4x4 slice. The times are simulated.
128 devices in a mesh: gx: 16 (over x, z_hi, core), gy: 8 (over z_lo, y).
Axes of the slice: x: 4, y: 4, z: 4 (z_hi: 2, z_lo: 2; z = z_hi * 2 + z_lo), core: 2. Of those that a mesh axis runs over, the one named last changes fastest.
Arguments:
- e_field: float32 [3, 24, 256, 2048], P(None, None, 'gx', 'gy'), may hold values from -6 to 6
- h_field: float32 [3, 24, 256, 2048], P(None, None, 'gx', 'gy'), may hold values from -6 to 6
- target: float32 [3, 24, 256, 2048], P(None, None, 'gx', 'gy'), may hold values from -6 to 6
- density: float32 [384, 32768], P('gx', 'gy'), may hold values from 0 to 1
- region_list: int32 [384, 8], P(None, 'gy'), may hold values from 0 to 383, as said below
- source_cells: int32 [3, 512], replicated, may hold values from 0 to 2047, as said below
- source_amp: float32 [2, 3, 512], replicated, may hold values from -6 to 6
Outputs:
- e_final: float32 [3, 24, 256, 2048], P(None, None, 'gx', 'gy')
- h_final: float32 [3, 24, 256, 2048], P(None, None, 'gx', 'gy')
- grad_density: float32 [384, 32768], P('gx', 'gy')
Inputs may be any that keep to these rules, and one draw needn't show every extreme that they name: `region_list`: column j lists, for the 24 rows of each optimizer shard along gx in turn, region ids t * 24 + k (plane k of the tile at gx index t in column j); each column holds every id once. One shard holds at most 3 rows of one tile, exactly 3 for some pairs in every column. `source_cells`: row 0 holds planes below 24, row 1 cells along x below 256, row 2 cells along y below 2048; cells may repeat.
All inputs are finite; a program needn't handle non-finite values.
Results may differ from a plain program's by a relative error of at most 0.00002.
Values sent between devices are 32-bit elements; how exact they have to be, the bound alone decides.
A program may use at most 576 MiB of HBM per device.

v0:
```python
import jax
import jax.numpy as jnp
from jax import lax
from jax.sharding import PartitionSpec as P

CX = 16
CY = 256
NZ = 24
STEPS = 2


STEP_DT = 0.5
SHARPNESS = 4.0
MIDPOINT = 0.5
EPS_LOW = 1.0
EPS_SPAN = 3.0


def shifted(x, axis, by):
    size = lax.axis_size(axis)
    pairs = [(i, i + by) for i in range(size) if 0 <= i + by < size]
    return lax.ppermute(x, axis, pairs)


def diff_ahead(values, rim_slab, which_axis):
    upper_side = jnp.concatenate(
        [lax.slice_in_dim(values, 1, values.shape[which_axis], axis=which_axis), rim_slab],
        axis=which_axis,
    )
    return upper_side - values


def diff_behind(values, rim_slab, which_axis):
    lower_side = jnp.concatenate(
        [rim_slab, lax.slice_in_dim(values, 0, values.shape[which_axis] - 1, axis=which_axis)],
        axis=which_axis,
    )
    return values - lower_side


def curl_ahead(fields):
    rims_across = shifted(fields[1:3, :, 0, :], "gx", -1)
    rims_lateral = shifted(jnp.stack([fields[0][:, :, 0], fields[2][:, :, 0]]), "gy", -1)
    zero_z = jnp.zeros_like(fields[0][:1])
    comp_x = diff_ahead(fields[2], rims_lateral[1][:, :, None], 2) - diff_ahead(
        fields[1], zero_z, 0
    )
    comp_y = diff_ahead(fields[0], zero_z, 0) - diff_ahead(fields[2], rims_across[1][:, None, :], 1)
    comp_z = diff_ahead(fields[1], rims_across[0][:, None, :], 1) - diff_ahead(
        fields[0], rims_lateral[0][:, :, None], 2
    )
    return jnp.stack([comp_x, comp_y, comp_z])


def curl_behind(fields):
    rims_across = shifted(fields[1:3, :, -1, :], "gx", 1)
    rims_lateral = shifted(jnp.stack([fields[0][:, :, -1], fields[2][:, :, -1]]), "gy", 1)
    zero_z = jnp.zeros_like(fields[0][:1])
    comp_x = diff_behind(fields[2], rims_lateral[1][:, :, None], 2) - diff_behind(
        fields[1], zero_z, 0
    )
    comp_y = diff_behind(fields[0], zero_z, 0) - diff_behind(
        fields[2], rims_across[1][:, None, :], 1
    )
    comp_z = diff_behind(fields[1], rims_across[0][:, None, :], 1) - diff_behind(
        fields[0], rims_lateral[0][:, :, None], 2
    )
    return jnp.stack([comp_x, comp_y, comp_z])


def smooth_rows(planes):
    padded = jnp.pad(planes, ((0, 0), (1, 1), (1, 1)))
    return 0.5 * planes + 0.125 * (
        padded[:, 2:, 1:-1] + padded[:, :-2, 1:-1] + padded[:, 1:-1, 2:] + padded[:, 1:-1, :-2]
    )


def project(filtered):
    norm_term = 2.0 * jnp.tanh(SHARPNESS * MIDPOINT)
    return (
        jnp.tanh(SHARPNESS * MIDPOINT) + jnp.tanh(SHARPNESS * (filtered - MIDPOINT))
    ) / norm_term


def project_slope(filtered):
    inner_tanh = jnp.tanh(SHARPNESS * (filtered - MIDPOINT))
    return SHARPNESS * (1.0 - inner_tanh * inner_tanh) / (2.0 * jnp.tanh(SHARPNESS * MIDPOINT))


def collect(design_rows, fold_fn):
    return fold_fn(
        jnp.zeros((NZ, CX * CY), jnp.float32),
        lax.all_gather(design_rows, "gx", axis=0, tiled=True),
        jnp.int32(0),
    )


def pick_rows(shard_rows, wanted_rows):
    row_count = shard_rows.shape[0]
    present = (wanted_rows >= 0) & (wanted_rows < row_count)
    picked = jnp.take(shard_rows, jnp.clip(wanted_rows, 0, row_count - 1), axis=0)
    return jnp.where(present[:, None], picked, 0.0)


def build_sources(source_cells, source_amp, local_x, local_y, extent_x, extent_y):
    empty = jnp.zeros((STEPS, 3, NZ, extent_x, extent_y), jnp.float32)
    return empty.at[:, :, source_cells[0], local_x, local_y].add(source_amp, mode="drop")


def body(e_field, h_field, target, density, region_list, source_cells, source_amp):
    shard_index = lax.axis_index("gx")
    column = lax.axis_index("gy")
    width_cells = CX * CY
    filtered = smooth_rows(density.reshape(NZ, CX, CY))
    projected = project(filtered).reshape(NZ, width_cells)
    flat_list = region_list[:, 0]
    plane_range = jnp.arange(NZ, dtype=jnp.int32)
    own_ids = lax.dynamic_slice_in_dim(flat_list, shard_index * NZ, NZ)
    all_rows = jnp.arange(flat_list.shape[0], dtype=jnp.int32)
    plane_hits = flat_list[None, :] == (shard_index * NZ + plane_range)[:, None]
    plane_row = jnp.sum(jnp.where(plane_hits, all_rows[None, :], 0), axis=1)

    def take_planes(running, shard_rows, first_row):
        return pick_rows(shard_rows, plane_row)

    def take_rows(running, shard_rows, first_row):
        return pick_rows(shard_rows, own_ids)

    rho_grid = collect(projected, take_planes).reshape(NZ, CX, CY)
    inv_eps = 1.0 / (EPS_LOW + EPS_SPAN * rho_grid)
    eps_grad = jnp.zeros((NZ, CX, CY), jnp.float32)
    local_x = source_cells[1] - shard_index * CX
    local_y = source_cells[2] - column * CY
    inside = (local_x >= 0) & (local_x < CX) & (local_y >= 0) & (local_y < CY)
    local_x = jnp.where(inside, local_x, CX)
    local_y = jnp.where(inside, local_y, CY)
    sources_all = build_sources(source_cells, source_amp, local_x, local_y, CX, CY)
    electric = e_field
    magnetic = h_field
    curls_saved = []
    for timestep in range(STEPS):
        magnetic = magnetic - STEP_DT * curl_ahead(electric)
        curl_now = curl_behind(magnetic)
        curls_saved.append(curl_now)
        electric = electric + STEP_DT * inv_eps[None] * curl_now + STEP_DT * sources_all[timestep]
    adjoint_e = electric - target
    adjoint_h = jnp.zeros_like(magnetic)
    for timestep in reversed(range(STEPS)):
        eps_grad = eps_grad + STEP_DT * jnp.sum(curls_saved[timestep] * adjoint_e, axis=0)
        adjoint_h = adjoint_h + curl_ahead(STEP_DT * inv_eps[None] * adjoint_e)
        if timestep > 0:
            adjoint_e = adjoint_e - STEP_DT * curl_behind(adjoint_h)
    plane_grads = (-EPS_SPAN * inv_eps * inv_eps * eps_grad).reshape(NZ, width_cells)
    row_grads = collect(plane_grads, take_rows).reshape(NZ, CX, CY) * project_slope(filtered)
    grad_density = smooth_rows(row_grads).reshape(NZ, width_cells)
    return (electric, magnetic, grad_density)


def solution(mesh):
    placed = (
        P(None, None, "gx", "gy"),
        P(None, None, "gx", "gy"),
        P(None, None, "gx", "gy"),
        P("gx", "gy"),
        P(None, "gy"),
        P(),
        P(),
    )
    return jax.shard_map(
        body,
        mesh=mesh,
        in_specs=placed,
        out_specs=(P(None, None, "gx", "gy"), P(None, None, "gx", "gy"), P("gx", "gy")),
        check_vma=False,
    )
```

profile of v0, /device:TPU:1, one launch (start us, length us, event | category | flops | bytes accessed | tf_op | source)
XLA Modules:
  0.0 532.0 jit_solution(13090918554191303477)
XLA Ops:
  7.2 1.1 copy.1200
  8.3 1.0 add_multiply_fusion.1
  9.4 1.0 copy.1201
  11.1 3.3 collective-permute-start.1
  15.5 1.3 collective-permute-start
  17.1 32.0 %broadcast_in_dim.61 = f32[2,3,24,16,256]{1,0,4,3,2:T(2,128)} broadcast(f32[]{:T(128)} %constant.10.clone.1), dimensions={} | broadcast | bytes 2359300 | tf_op jit(solution)/shard_map/broadcast_in_dim | solution.py:106
  49.2 48.3 %scatter_fusion = f32[2,3,24,16,256]{1,0,4,3,2:T(2,128)} fusion(f32[2,3,24,16,256]{1,0,4,3,2:T(2,128)} %broadcast_in_dim.61, s32[512]{0:T(512)S(1)} %bitcast.268, f32[512,2,3]{2,1,0:T(2,128)S(1)} %copy.1151), kind=kCustom, calls=%fused_computation.2 | custom fusion | flops 3072 | bytes 43008 | tf_op jit(solution)/shard_map/scatter-add | solution.py:107
  97.4 98.1 %fusion.55 = (f32[1,3,24,16,256]{1,0,4,3,2:T(1,128)}, f32[1,3,24,16,256]{1,0,4,3,2:T(1,128)}) fusion(f32[2,3,24,16,256]{1,0,4,3,2:T(2,128)} %scatter_fusion), kind=kLoop, calls=%fused_computation.202 | loop fusion | bytes 4718592 | tf_op jit(solution)/shard_map/slice | solution.py:145
  199.0 62.3 %copy.1198 = f32[1,3,24,16,256]{4,3,2,1,0:T(8,128)} copy(f32[1,3,24,16,256]{1,0,4,3,2:T(1,128)} %get-tuple-element.58) | data formatting | bytes 2359296
  261.3 62.3 %copy.1197 = f32[1,3,24,16,256]{4,3,2,1,0:T(8,128)} copy(f32[1,3,24,16,256]{1,0,4,3,2:T(1,128)} %get-tuple-element.57) | data formatting | bytes 2359296
  326.8 1.0 slice_bitcast_fusion.9
  328.6 1.1 copy.1144
  329.7 1.7 slice.518
  331.4 1.1 copy.1143
  332.5 4.5 collective-permute-start.2
  337.0 1.8 slice_bitcast_fusion.7
  338.8 0.9 slice_bitcast_fusion.20
  341.2 6.8 %collective-permute-start.3 = (f32[2,24,256]{2,0,1:T(2,128)}, f32[2,24,256]{2,0,1:T(2,128)}, u32[]{:S(2)}, u32[]{:S(2)}) collective-permute-start(f32[2,24,256]{2,0,1:T(2,128)} %bitcast.259), channel_id=1, source_target_pairs={{0,8},{8,16},{16,24},{24,32},{32,40},{40,48},{48,56},{56,64},{64,7... | collective-permute-start | bytes 147464 | tf_op jit(solution)/shard_map/ppermute | solution.py:22
  349.7 0.9 slice_bitcast_fusion.41
  350.7 2.1 fusion.28
  352.8 1.2 fusion.25
  354.1 3.8 gather_fusion
  358.2 1.2 copy-done.2
  359.5 1.6 bitcast_add_fusion.1
  362.9 0.9 slice_bitcast_fusion.18
  364.5 1.9 collective-permute-start.5
  366.5 1.1 copy.1154
  367.6 1.1 copy.1153
  368.7 1.3 collective-permute-start.4
  370.7 2.7 collective-permute-done.4
  373.5 0.9 copy.1160
  376.1 1.2 fusion.33
  377.8 0.9 copy-done.5
  379.3 1.0 slice.551
  380.2 0.9 slice_bitcast_fusion.16
  382.0 1.1 copy.1162
  383.1 1.1 copy.1161
  384.2 3.3 collective-permute-start.6
  389.0 7.1 %collective-permute-start.7 = (f32[2,24,256]{2,0,1:T(2,128)}, f32[2,24,256]{2,0,1:T(2,128)}, u32[]{:S(2)}, u32[]{:S(2)}) collective-permute-start(f32[2,24,256]{2,0,1:T(2,128)} %bitcast.258), channel_id=1, source_target_pairs={{0,8},{8,16},{16,24},{24,32},{32,40},{40,48},{48,56},{56,64},{64,7... | collective-permute-start | bytes 147464 | tf_op jit(solution)/shard_map/ppermute | solution.py:22
  396.1 0.9 copy.1168
  397.9 0.9 slice_bitcast_fusion.37
  398.8 1.2 fusion.38
  402.2 1.8 broadcast_multiply_fusion
  404.8 1.1 fusion.56
  405.9 0.9 slice_bitcast_fusion.14
  406.9 0.9 slice.576
  408.4 1.9 collective-permute-start.8
  410.7 1.3 collective-permute-start.9
  412.0 1.0 fusion.57
  413.7 2.6 collective-permute-done.9
  418.1 0.9 copy.1182
  418.9 1.4 slice_bitcast_fusion.45
  420.3 2.3 fusion.39
  423.4 1.1 copy.1176
  425.3 1.1 copy.1175
  426.4 5.6 %collective-permute-start.10 = (f32[2,24,16]{1,2,0:T(8,128)S(1)}, f32[2,24,16]{1,2,0:T(8,128)S(1)}, u32[]{:S(2)}, u32[]{:S(2)}) collective-permute-start(f32[2,24,16]{1,2,0:T(8,128)S(1)} %pad_maximum_fusion.8), channel_id=1, source_target_pairs={{0,1},{1,2},{2,3},{3,4},{4,5},{5,6},{6,7},{8,9},{9,10},{10,11},{11... | collective-permute-start | bytes 9224 | tf_op jit(solution)/shard_map/ppermute | solution.py:22
  432.8 1.4 fusion.44
  435.8 6.4 %collective-permute-start.11 = (f32[2,24,256]{2,1,0:T(8,128)S(1)}, f32[2,24,256]{2,1,0:T(8,128)S(1)}, u32[]{:S(2)}, u32[]{:S(2)}) collective-permute-start(f32[2,24,256]{2,1,0:T(8,128)S(1)} %bitcast.290), channel_id=1, source_target_pairs={{0,8},{8,16},{16,24},{24,32},{32,40},{40,48},{48,56},{56,64},{64,7... | collective-permute-start | bytes 147464 | tf_op jit(solution)/shard_map/ppermute | solution.py:22
  442.3 0.9 copy.1177
  444.1 1.9 fusion.42
  447.8 0.9 fusion.5
  448.9 70.3 %all-gather.5.cloned.1.call-done = f32[384,4096]{1,0:T(8,128)} async-done(((f32[24,4096]{1,0:T(8,128)}), f32[384,4096]{1,0:T(8,128)}) %all-gather.5.cloned.1.call-update) | async-done | bytes 6291472 | tf_op jit(solution)/shard_map/all_gather | solution.py:93
  519.2 3.6 gather_fusion.1
  524.2 1.0 copy.1205
  (206 shorter events, 36.7 us)
Async XLA Ops:
  7.2 346.9 %all-gather.3.cloned.1.call-start = ((), (), s32[]{:S(2)}) async-start(), calls=%async_computation | async-start | bytes 6684672 | tf_op jit(solution)/shard_map/all_gather | solution.py:93
  8.3 2.1 copy-start
  10.4 508.8 %all-gather.5.cloned.1.call-start = ((), (), s32[]{:S(2)}) async-start(), calls=%async_computation.1 | async-start | bytes 6684672 | tf_op jit(solution)/shard_map/all_gather | solution.py:93
  11.1 312.9 %collective-permute-start.1 = (f32[2,24,256]{2,1,0:T(8,128)}, f32[2,24,256]{2,1,0:T(8,128)}, u32[]{:S(2)}, u32[]{:S(2)}) collective-permute-start(f32[2,24,256]{2,1,0:T(8,128)} %bitcast.255), channel_id=1, source_target_pairs={{8,0},{16,8},{24,16},{32,24},{40,32},{48,40},{56,48},{64,56},{72,6... | collective-permute-start | bytes 147464 | tf_op jit(solution)/shard_map/ppermute | solution.py:22
  14.5 2.3 copy-start.37
  14.5 2.6 copy-start.42
  15.5 308.1 %collective-permute-start = (f32[2,24,16]{1,2,0:T(8,128)}, f32[2,24,16]{1,2,0:T(8,128)S(1)}, u32[]{:S(2)}, u32[]{:S(2)}) collective-permute-start(f32[2,24,16]{1,2,0:T(8,128)} %pad_maximum_fusion.3), channel_id=1, source_target_pairs={{1,0},{2,1},{3,2},{4,3},{5,4},{6,5},{7,6},{9,8},{10,9},{11,10},{12... | collective-permute-start | bytes 9224 | tf_op jit(solution)/shard_map/ppermute | solution.py:22
  97.4 98.1 %copy-start.43 = (s32[384,1]{0,1:T(1,128)S(1)}, s32[384,1]{0,1:T(1,128)}, u32[]{:S(2)}) copy-start(s32[384,1]{0,1:T(1,128)} %param.13) | copy-start | bytes 4612
  324.0 1.1 copy-start.22
  324.0 1.1 copy-start.29
  325.1 0.8 copy-start.14
  325.2 1.4 copy-start.4
  332.5 7.2 %copy-start.23 = (f32[24,16,256]{2,1,0:T(8,128)S(1)}, f32[24,16,256]{2,1,0:T(8,128)}, u32[]{:S(2)}) copy-start(f32[24,16,256]{2,1,0:T(8,128)} %get-tuple-element.86) | copy-start | bytes 1179652
  332.5 15.5 %collective-permute-start.2 = (f32[2,24,16]{1,2,0:T(8,128)S(1)}, f32[2,24,16]{1,2,0:T(8,128)S(1)}, u32[]{:S(2)}, u32[]{:S(2)}) collective-permute-start(f32[2,24,16]{1,2,0:T(8,128)S(1)} %pad_maximum_fusion.4), channel_id=1, source_target_pairs={{0,1},{1,2},{2,3},{3,4},{4,5},{5,6},{6,7},{8,9},{9,10},{10,11},{11... | collective-permute-start | bytes 9224 | tf_op jit(solution)/shard_map/ppermute | solution.py:22
  341.2 8.6 %collective-permute-start.3 = (f32[2,24,256]{2,0,1:T(2,128)}, f32[2,24,256]{2,0,1:T(2,128)}, u32[]{:S(2)}, u32[]{:S(2)}) collective-permute-start(f32[2,24,256]{2,0,1:T(2,128)} %bitcast.259), channel_id=1, source_target_pairs={{0,8},{8,16},{16,24},{24,32},{32,40},{40,48},{48,56},{56,64},{64,7... | collective-permute-start | bytes 147464 | tf_op jit(solution)/shard_map/ppermute | solution.py:22
  349.7 3.1 copy-start.30
  349.7 3.1 copy-start.31
  349.7 3.1 copy-start.34
  354.1 3.8 copy-start.38
  354.1 3.8 copy-start.40
  357.8 3.2 copy-start.16
  357.8 1.6 copy-start.2
  357.8 1.6 copy-start.18
  358.2 2.9 copy-start.6
  364.5 10.6 %collective-permute-start.5 = (f32[2,24,256]{2,1,0:T(8,128)}, f32[2,24,256]{2,1,0:T(8,128)}, u32[]{:S(2)}, u32[]{:S(2)}) collective-permute-start(f32[2,24,256]{2,1,0:T(8,128)} %bitcast.257), channel_id=1, source_target_pairs={{8,0},{16,8},{24,16},{32,24},{40,32},{48,40},{56,48},{64,56},{72,6... | collective-permute-start | bytes 147464 | tf_op jit(solution)/shard_map/ppermute | solution.py:22
  368.7 4.8 collective-permute-start.4
  375.2 2.2 copy-start.25
  375.2 2.2 copy-start.26
  375.2 2.2 copy-start.33
  377.4 1.3 copy-start.5
  377.4 1.3 copy-start.15
  379.1 20.9 %copy-start.1 = (f32[3,24,16,256]{3,2,1,0:T(8,128)}, f32[3,24,16,256]{3,2,1,0:T(8,128)S(1)}, u32[]{:S(2)}) copy-start(f32[3,24,16,256]{3,2,1,0:T(8,128)S(1)} %fusion.1) | copy-start | bytes 3538948
  384.2 11.9 %collective-permute-start.6 = (f32[2,24,16]{1,2,0:T(8,128)S(1)}, f32[2,24,16]{1,2,0:T(8,128)S(1)}, u32[]{:S(2)}, u32[]{:S(2)}) collective-permute-start(f32[2,24,16]{1,2,0:T(8,128)S(1)} %pad_maximum_fusion.6), channel_id=1, source_target_pairs={{0,1},{1,2},{2,3},{3,4},{4,5},{5,6},{6,7},{8,9},{9,10},{10,11},{11... | collective-permute-start | bytes 9224 | tf_op jit(solution)/shard_map/ppermute | solution.py:22
  389.0 8.8 %collective-permute-start.7 = (f32[2,24,256]{2,0,1:T(2,128)}, f32[2,24,256]{2,0,1:T(2,128)}, u32[]{:S(2)}, u32[]{:S(2)}) collective-permute-start(f32[2,24,256]{2,0,1:T(2,128)} %bitcast.258), channel_id=1, source_target_pairs={{0,8},{8,16},{16,24},{24,32},{32,40},{40,48},{48,56},{56,64},{64,7... | collective-permute-start | bytes 147464 | tf_op jit(solution)/shard_map/ppermute | solution.py:22
  397.8 2.2 copy-start.27
  397.8 2.2 copy-start.28
  397.8 2.2 copy-start.35
  400.0 0.8 copy-start.12
  400.1 1.5 copy-start.3
  400.1 1.7 copy-start.7
  400.1 2.1 copy-start.32
  400.5 3.5 copy-start.8
  400.5 3.5 copy-start.10
  405.9 4.6 copy-start.36
  408.4 10.5 %collective-permute-start.8 = (f32[2,24,256]{2,1,0:T(8,128)}, f32[2,24,256]{2,1,0:T(8,128)}, u32[]{:S(2)}, u32[]{:S(2)}) collective-permute-start(f32[2,24,256]{2,1,0:T(8,128)} %bitcast.256), channel_id=1, source_target_pairs={{8,0},{16,8},{24,16},{32,24},{40,32},{48,40},{56,48},{64,56},{72,6... | collective-permute-start | bytes 147464 | tf_op jit(solution)/shard_map/ppermute | solution.py:22
  410.7 5.7 %collective-permute-start.9 = (f32[2,24,16]{1,2,0:T(8,128)S(1)}, f32[2,24,16]{1,2,0:T(8,128)S(1)}, u32[]{:S(2)}, u32[]{:S(2)}) collective-permute-start(f32[2,24,16]{1,2,0:T(8,128)S(1)} %pad_maximum_fusion.7), channel_id=1, source_target_pairs={{1,0},{2,1},{3,2},{4,3},{5,4},{6,5},{7,6},{9,8},{10,9},{11,10},{12... | collective-permute-start | bytes 9224 | tf_op jit(solution)/shard_map/ppermute | solution.py:22
  426.4 15.8 %collective-permute-start.10 = (f32[2,24,16]{1,2,0:T(8,128)S(1)}, f32[2,24,16]{1,2,0:T(8,128)S(1)}, u32[]{:S(2)}, u32[]{:S(2)}) collective-permute-start(f32[2,24,16]{1,2,0:T(8,128)S(1)} %pad_maximum_fusion.8), channel_id=1, source_target_pairs={{0,1},{1,2},{2,3},{3,4},{4,5},{5,6},{6,7},{8,9},{9,10},{10,11},{11... | collective-permute-start | bytes 9224 | tf_op jit(solution)/shard_map/ppermute | solution.py:22
  435.8 8.2 %collective-permute-start.11 = (f32[2,24,256]{2,1,0:T(8,128)S(1)}, f32[2,24,256]{2,1,0:T(8,128)S(1)}, u32[]{:S(2)}, u32[]{:S(2)}) collective-permute-start(f32[2,24,256]{2,1,0:T(8,128)S(1)} %bitcast.290), channel_id=1, source_target_pairs={{0,8},{8,16},{16,24},{24,32},{32,40},{40,48},{48,56},{56,64},{64,7... | collective-permute-start | bytes 147464 | tf_op jit(solution)/shard_map/ppermute | solution.py:22
  444.1 2.0 copy-start.9
  444.1 2.0 copy-start.11
  444.1 2.0 copy-start.13
  444.1 2.0 copy-start.19
  444.1 2.0 copy-start.20
  444.1 2.0 copy-start.21
  446.8 1.0 copy-start.17
  446.8 1.0 copy-start.39
  446.8 1.0 copy-start.41
  446.9 1.9 copy-start.44
  522.8 1.0 copy-start.24
Sparse Core Ops, SparseCore 0:
  10.5 67.4 all-gather.2
  448.8 70.3 all-gather.4
where the time goes:
time: 538 us; the launch traced here: 532 us
  local copies, waits for them, and re-layouts  326 us (61%)
  waiting for transfers between devices  75.7 us (14%)
  other arithmetic  70.6 us (13%)
  starting transfers between devices  44.7 us (8%)
  between operations  15.1 us (3%)
    unnamed x103, local copies, waits for them, and re-layouts  137 us
    slice x1, local copies, waits for them, and re-layouts, body(): sources_all[timestep]  98.1 us
    all_gather x2, waiting for transfers between devices, collect(): lax.all_gather(design_rows, 'gx', axis=0, tiled=True)  70.3 us
    scatter-add x1, other arithmetic, build_sources(): empty.at[:, :, source_cells[0], local_x, local_y]  48.3 us
    ppermute x12, starting transfers between devices, shifted(): return lax.ppermute(x, axis, pairs)  44.7 us
    broadcast_in_dim x1, local copies, waits for them, and re-layouts, build_sources(): empty = jnp.zeros((STEPS, 3, NZ, extent_x, extent_y), jnp.float32)  32 us
  transfers between devices with their start and end apart: 14, of which 3 were waited for; matrix products, arithmetic and copies ran while one was open for 65% of the time, Pallas kernels for 0%

commit v1 on v0

v1 whole, which is shorter than its diff:
```python
import jax
import jax.numpy as jnp
from jax import lax
from jax.experimental import pallas as pl
from jax.experimental.pallas import tpu as pltpu
from jax.sharding import PartitionSpec as P

CX = 16
CY = 256
NZ = 24
STEPS = 2
CAP = 3
NSRC = 512
WIDTH = CX * CY

STEP_DT = 0.5
SHARPNESS = 4.0
MIDPOINT = 0.5
EPS_LOW = 1.0
EPS_SPAN = 3.0
TANH_MID = 0.9640275800758169

F32 = jnp.float32
MESH = pl.DeviceIdType.MESH


def index_tables(region_list, n_gx):
    me = lax.axis_index("gx")
    ids = region_list[:, 0].reshape(n_gx, NZ)
    tile, plane = ids // NZ, ids % NZ
    place = jnp.arange(NZ, dtype=jnp.int32)
    earlier = place[None, :] < place[:, None]
    rank = jnp.sum(
        ((tile[:, :, None] == tile[:, None, :]) & earlier[None]).astype(jnp.int32), axis=2
    )
    own_tile = lax.dynamic_slice_in_dim(tile, me, 1)[0]
    own_rank = lax.dynamic_slice_in_dim(rank, me, 1)[0]
    own_slot = own_tile * CAP + own_rank
    slots = jnp.arange(n_gx * CAP, dtype=jnp.int32)
    send_rows = jnp.sum(jnp.where(own_slot[None, :] == slots[:, None], place[None, :], 0), axis=1)
    shard_slot = jnp.arange(n_gx, dtype=jnp.int32)[:, None] * CAP + rank
    shard_slot_here = jnp.where(tile == me, shard_slot, -1)
    send_planes = jnp.sum(
        jnp.where(shard_slot_here[None] == slots[:, None, None], plane[None], 0), axis=(1, 2)
    )
    take_planes = jnp.sum(
        jnp.where(ids[None] == (me * NZ + place)[:, None, None], shard_slot[None], 0), axis=(1, 2)
    )
    return jnp.concatenate([send_rows, send_planes, take_planes, own_slot]).astype(jnp.int32)


def kernel(n_gx, n_gy, idx, cells, amp, e_hbm, h_hbm, t_hbm, d_hbm, e_out, h_out, g_out,
           E, H, T, D, SL, C1, C2, G, S, L, ROW, INV, EG, SEND1, RECV1, SEND2, RECV2,
           XS, XR, YS, YR, local_sem, row_send, row_recv, x_send, x_recv, y_send, y_recv):
    gx = lax.axis_index("gx")
    gy = lax.axis_index("gy")
    n_slots = n_gx * CAP
    row_lines = ROW.reshape(2 * NZ * CX, 128)

    barrier = pltpu.get_barrier_semaphore()
    for d in range(1, n_gx):
        pl.semaphore_signal(barrier, inc=1, device_id=(lax.rem(gx + d, n_gx), gy), device_id_type=MESH)
    for d in (1, n_gy - 1):
        pl.semaphore_signal(barrier, inc=1, device_id=(gx, lax.rem(gy + d, n_gy)), device_id_type=MESH)

    load_d = pltpu.make_async_copy(d_hbm, D.at[:, CY:CY + WIDTH], local_sem.at[0])
    load_e = pltpu.make_async_copy(e_hbm, E.at[:, 0:NZ], local_sem.at[1])
    load_h = pltpu.make_async_copy(h_hbm, H.at[:, 1:NZ + 1], local_sem.at[2])
    load_t = pltpu.make_async_copy(t_hbm, T, local_sem.at[3])
    load_d.start()
    load_e.start()
    load_h.start()
    load_t.start()

    zero_plane = jnp.zeros((CX, CY), F32)
    for c in range(3):
        E[c, NZ] = zero_plane
        G[c, NZ] = zero_plane
        H[c, 0] = zero_plane
    D[:, 0:CY] = jnp.zeros((NZ, CY), F32)
    D[:, CY + WIDTH:] = jnp.zeros((NZ, CY), F32)

    lane_wide = lax.broadcasted_iota(jnp.int32, (NZ, CY), 1)
    sub = lax.broadcasted_iota(jnp.int32, (CX, CY), 0)
    lane128 = lax.broadcasted_iota(jnp.int32, (CX, 128), 1)
    first_row, last_row = sub == 0, sub == CX - 1
    first_lane, last_lane = lane128 == 0, lane128 == 127
    wide_first, wide_last = lane_wide == 0, lane_wide == CY - 1

    def smooth(ref, a):
        at = pl.multiple_of((a + 1) * CY, CY)
        mid = ref[:, pl.ds(at, CY)]
        low = ref[:, pl.ds(pl.multiple_of(at - CY, CY), CY)]
        high = ref[:, pl.ds(pl.multiple_of(at + CY, CY), CY)]
        right = jnp.where(wide_last, 0.0, pltpu.roll(mid, CY - 1, 1))
        left = jnp.where(wide_first, 0.0, pltpu.roll(mid, 1, 1))
        return 0.5 * mid + 0.125 * (high + low + right + left)

    load_d.wait()

    def rows_in(a, carry):
        filtered = smooth(D, a)
        inner = jnp.tanh(SHARPNESS * (filtered - MIDPOINT))
        SL[:, pl.ds(pl.multiple_of(a * CY, CY), CY)] = (
            SHARPNESS * (1.0 - inner * inner) / (2.0 * TANH_MID)
        )
        projected = (TANH_MID + inner) / (2.0 * TANH_MID)
        for half in range(2):
            row_lines[pl.ds(half * NZ * CX + a, NZ, stride=CX), :] = projected[:, half * 128:half * 128 + 128]
        return carry

    lax.fori_loop(0, CX, rows_in, 0)

    def pack_rows(slot, carry):
        row = idx[slot]
        SEND1[slot, :, 0:128] = ROW[row]
        SEND1[slot, :, 128:256] = ROW[NZ + row]
        return carry

    lax.fori_loop(0, n_slots, pack_rows, 0)

    def pack_low(acc, z, k, fx, fy, fz):
        XS[k, pl.ds(z, 1), :] = fy[0:1, :]
        XS[k, pl.ds(NZ + z, 1), :] = fz[0:1, :]
        acc = jnp.where(lane128 == z, pltpu.roll(fx[:, 0:128], z, 1), acc)
        return jnp.where(lane128 == NZ + z, pltpu.roll(fz[:, 0:128], NZ + z, 1), acc)

    def pack_high(acc, z, k, fx, fy, fz):
        XS[k, pl.ds(z, 1), :] = fy[CX - 1:CX, :]
        XS[k, pl.ds(NZ + z, 1), :] = fz[CX - 1:CX, :]
        acc = jnp.where(lane128 == z, pltpu.roll(fx[:, 128:256], z + 1, 1), acc)
        return jnp.where(lane128 == NZ + z, pltpu.roll(fz[:, 128:256], NZ + z + 1, 1), acc)

    def rim_copies(k, down):
        step_x = n_gx - 1 if down else 1
        step_y = n_gy - 1 if down else 1
        across = pltpu.make_async_remote_copy(
            src_ref=XS.at[k], dst_ref=XR.at[k], send_sem=x_send.at[k], recv_sem=x_recv.at[k],
            device_id=(lax.rem(gx + step_x, n_gx), gy), device_id_type=MESH)
        lateral = pltpu.make_async_remote_copy(
            src_ref=YS.at[k], dst_ref=YR.at[k], send_sem=y_send.at[k], recv_sem=y_recv.at[k],
            device_id=(gx, lax.rem(gy + step_y, n_gy)), device_id_type=MESH)
        return across, lateral

    def start_rims(k, down):
        across, lateral = rim_copies(k, down)
        across.start()
        lateral.start()

    def finish_rims(k, down):
        across, lateral = rim_copies(k, down)
        across.wait()
        lateral.wait()
        edge_x = gx == (n_gx - 1 if down else 0)
        edge_y = gy == (n_gy - 1 if down else 0)
        XR[k] = XR[k] * jnp.where(edge_x, 0.0, 1.0)
        YR[k] = YR[k] * jnp.where(edge_y, 0.0, 1.0)

    blank = jnp.zeros((CX, 128), F32)

    def curl_ahead(F, z, k):
        fx, fy, fz = F[0, z], F[1, z], F[2, z]
        rim_y = XR[k, pl.ds(z, 1), :]
        rim_z = XR[k, pl.ds(NZ + z, 1), :]
        lat = YR[k]
        lat_x = pltpu.roll(lat, 127 - z, 1)
        lat_z = pltpu.roll(lat, 127 - NZ - z, 1)

        def up_x(v, rim):
            return jnp.where(last_row, rim, pltpu.roll(v, CX - 1, 0))

        def up_y(v, lateral):
            r = pltpu.roll(v, CY - 1, 1)
            return jnp.concatenate([r[:, 0:128], jnp.where(last_lane, lateral, r[:, 128:256])], axis=1)

        cx = (up_y(fz, lat_z) - fz) - (F[1, z + 1] - fy)
        cy = (F[0, z + 1] - fx) - (up_x(fz, rim_z) - fz)
        cz = (up_x(fy, rim_y) - fy) - (up_y(fx, lat_x) - fx)
        return cx, cy, cz

    def curl_behind(F, z, k):
        fx, fy, fz = F[0, z + 1], F[1, z + 1], F[2, z + 1]
        rim_y = XR[k, pl.ds(z, 1), :]
        rim_z = XR[k, pl.ds(NZ + z, 1), :]
        lat = YR[k]
        lat_x = pltpu.roll(lat, lax.rem(128 - z, 128), 1)
        lat_z = pltpu.roll(lat, 128 - NZ - z, 1)

        def dn_x(v, rim):
            return jnp.where(first_row, rim, pltpu.roll(v, 1, 0))

        def dn_y(v, lateral):
            r = pltpu.roll(v, 1, 1)
            return jnp.concatenate([jnp.where(first_lane, lateral, r[:, 0:128]), r[:, 128:256]], axis=1)

        cx = (fz - dn_y(fz, lat_z)) - (fy - F[1, z])
        cy = (fx - F[0, z]) - (fz - dn_x(fz, rim_z))
        cz = (fy - dn_x(fy, rim_y)) - (fx - dn_y(fx, lat_x))
        return cx, cy, cz

    load_e.wait()

    def pack_e0(z, acc):
        return pack_low(acc, z, 0, E[0, z], E[1, z], E[2, z])

    YS[0] = lax.fori_loop(0, NZ, pack_e0, blank)

    pl.semaphore_wait(barrier, n_gx + 1)
    start_rims(0, True)

    def row_copy(send, recv, d, which):
        peer = lax.rem(gx + d, n_gx)
        return pltpu.make_async_remote_copy(
            src_ref=send.at[pl.ds(peer * CAP, CAP)], dst_ref=recv.at[pl.ds(gx * CAP, CAP)],
            send_sem=row_send.at[which, d], recv_sem=row_recv.at[which, d],
            device_id=(peer, gy), device_id_type=MESH)

    for d in range(1, n_gx):
        row_copy(SEND1, RECV1, d, 0).start()
    for s in range(CAP):
        RECV1[gx * CAP + s] = SEND1[gx * CAP + s]

    load_h.wait()
    finish_rims(0, True)

    def h_first(z, acc):
        cx, cy, cz = curl_ahead(E, z, 0)
        hx = H[0, z + 1] - STEP_DT * cx
        hy = H[1, z + 1] - STEP_DT * cy
        hz = H[2, z + 1] - STEP_DT * cz
        H[0, z + 1] = hx
        H[1, z + 1] = hy
        H[2, z + 1] = hz
        return pack_high(acc, z, 1, hx, hy, hz)

    YS[1] = lax.fori_loop(0, NZ, h_first, blank)
    start_rims(1, False)

    local_x = cells[1:2, :] - gx * CX
    inside = (local_x >= 0) & (local_x < CX)
    where_zx = jnp.where(inside, cells[0:1, :] * CX + local_x, -1)
    where_y = cells[2:3, :] - gy * CY
    sub_src = lax.broadcasted_iota(jnp.int32, (CX, NSRC), 0)

    def build_hits(z, carry):
        hit = sub_src == where_zx - z * CX
        L[pl.ds(pl.multiple_of(z * CX, CX), CX), :] = jnp.where(hit, 1.0, 0.0).astype(jnp.bfloat16)
        return carry

    lax.fori_loop(0, NZ, build_hits, 0)
    hit_y = lax.broadcasted_iota(jnp.int32, (CY, NSRC), 0) == where_y

    for n in range(STEPS):
        for c in range(3):
            row = amp[n, c:c + 1, :]
            high = row.astype(jnp.bfloat16).astype(F32)
            rest = row - high
            mid = rest.astype(jnp.bfloat16).astype(F32)
            low = rest - mid
            total = None
            for part in (high, mid, low):
                cols = jnp.where(hit_y, part, 0.0).astype(jnp.bfloat16)
                term = lax.dot_general(L[...], cols, (((1,), (1,)), ((), ())),
                                       preferred_element_type=F32)
                total = term if total is None else total + term
            S[n * 3 + c] = total.reshape(NZ, CX, CY)

    finish_rims(1, False)

    def c_first(z, carry):
        cx, cy, cz = curl_behind(H, z, 1)
        C1[0, z] = cx
        C1[1, z] = cy
        C1[2, z] = cz
        return carry

    lax.fori_loop(0, NZ, c_first, 0)

    for d in range(1, n_gx):
        row_copy(SEND1, RECV1, d, 0).wait()

    def e_first(z, acc):
        inv = 1.0 / (EPS_LOW + EPS_SPAN * RECV1[idx[2 * n_slots + z]])
        INV[z] = inv
        new = []
        for c in range(3):
            value = E[c, z] + STEP_DT * inv * C1[c, z] + STEP_DT * S[c, z]
            E[c, z] = value
            new.append(value)
        return pack_low(acc, z, 2, *new)

    YS[2] = lax.fori_loop(0, NZ, e_first, blank)
    start_rims(2, True)
    finish_rims(2, True)

    def h_second(z, acc):
        curls = curl_ahead(E, z, 2)
        new = []
        for c in range(3):
            value = H[c, z + 1] - STEP_DT * curls[c]
            H[c, z + 1] = value
            new.append(value)
        return pack_high(acc, z, 3, *new)

    YS[3] = lax.fori_loop(0, NZ, h_second, blank)
    start_rims(3, False)
    save_h = pltpu.make_async_copy(H.at[:, 1:NZ + 1], h_out, local_sem.at[4])
    save_h.start()
    load_t.wait()
    finish_rims(3, False)

    def e_second(z, acc):
        curls = curl_behind(H, z, 3)
        inv = INV[z]
        half_inv = STEP_DT * inv
        grad = None
        new = []
        for c in range(3):
            value = E[c, z] + half_inv * curls[c] + STEP_DT * S[3 + c, z]
            E[c, z] = value
            misfit = value - T[c, z]
            T[c, z] = misfit
            grad = curls[c] * misfit if grad is None else grad + curls[c] * misfit
            value = half_inv * misfit
            G[c, z] = value
            new.append(value)
        EG[z] = grad
        return pack_low(acc, z, 4, *new)

    YS[4] = lax.fori_loop(0, NZ, e_second, blank)
    start_rims(4, True)
    save_e = pltpu.make_async_copy(E.at[:, 0:NZ], e_out, local_sem.at[5])
    save_e.start()
    finish_rims(4, True)

    for c in range(3):
        C2[c, 0] = zero_plane

    def adjoint_h(z, acc):
        curls = curl_ahead(G, z, 4)
        for c in range(3):
            C2[c, z + 1] = curls[c]
        return pack_high(acc, z, 5, *curls)

    YS[5] = lax.fori_loop(0, NZ, adjoint_h, blank)
    start_rims(5, False)
    finish_rims(5, False)

    def adjoint_e(z, carry):
        curls = curl_behind(C2, z, 5)
        grad = EG[z]
        for c in range(3):
            grad = grad + C1[c, z] * (T[c, z] - STEP_DT * curls[c])
        inv = INV[z]
        EG[z] = (-EPS_SPAN * STEP_DT) * (inv * inv) * grad
        return carry

    lax.fori_loop(0, NZ, adjoint_e, 0)

    def pack_planes(slot, carry):
        SEND2[slot] = EG[idx[n_slots + slot]]
        return carry

    lax.fori_loop(0, n_slots, pack_planes, 0)
    for d in range(1, n_gx):
        row_copy(SEND2, RECV2, d, 1).start()
    for s in range(CAP):
        RECV2[gx * CAP + s] = SEND2[gx * CAP + s]
    for d in range(1, n_gx):
        row_copy(SEND2, RECV2, d, 1).wait()

    def unpack(r, carry):
        plane = RECV2[idx[2 * n_slots + NZ + r]]
        ROW[r] = plane[:, 0:128]
        ROW[NZ + r] = plane[:, 128:256]
        return carry

    lax.fori_loop(0, NZ, unpack, 0)

    def scale(a, carry):
        own = SL[:, pl.ds(pl.multiple_of(a * CY, CY), CY)]
        parts = [row_lines[pl.ds(half * NZ * CX + a, NZ, stride=CX), :] for half in range(2)]
        D[:, pl.ds(pl.multiple_of((a + 1) * CY, CY), CY)] = jnp.concatenate(parts, axis=1) * own
        return carry

    lax.fori_loop(0, CX, scale, 0)

    def rows_out(a, carry):
        SL[:, pl.ds(pl.multiple_of(a * CY, CY), CY)] = smooth(D, a)
        return carry

    lax.fori_loop(0, CX, rows_out, 0)
    save_g = pltpu.make_async_copy(SL, g_out, local_sem.at[6])
    save_g.start()
    save_h.wait()
    save_e.wait()
    save_g.wait()


def solution(mesh):
    n_gx, n_gy = mesh.shape["gx"], mesh.shape["gy"]
    n_slots = n_gx * CAP
    placed = (
        P(None, None, "gx", "gy"),
        P(None, None, "gx", "gy"),
        P(None, None, "gx", "gy"),
        P("gx", "gy"),
        P(None, "gy"),
        P(),
        P(),
    )
    field = (3, NZ, CX, CY)
    padded = (3, NZ + 1, CX, CY)

    def body(e_field, h_field, target, density, region_list, source_cells, source_amp):
        idx = index_tables(region_list, n_gx)
        any_spec = pl.BlockSpec(memory_space=pl.ANY)
        vmem = pl.BlockSpec(memory_space=pltpu.VMEM)
        smem = pl.BlockSpec(memory_space=pltpu.SMEM)

        def run(*refs):
            kernel(n_gx, n_gy, *refs)

        dma = pltpu.SemaphoreType.DMA
        return pl.pallas_call(
            run,
            name="yee_adjoint",
            out_shape=(
                jax.ShapeDtypeStruct(field, F32),
                jax.ShapeDtypeStruct(field, F32),
                jax.ShapeDtypeStruct((NZ, WIDTH), F32),
            ),
            in_specs=[smem, vmem, vmem, any_spec, any_spec, any_spec, any_spec],
            out_specs=(any_spec, any_spec, any_spec),
            scratch_shapes=[
                pltpu.VMEM(padded, F32),
                pltpu.VMEM(padded, F32),
                pltpu.VMEM(field, F32),
                pltpu.VMEM((NZ, WIDTH + 2 * CY), F32),
                pltpu.VMEM((NZ, WIDTH), F32),
                pltpu.VMEM(field, F32),
                pltpu.VMEM(padded, F32),
                pltpu.VMEM(padded, F32),
                pltpu.VMEM((STEPS * 3, NZ, CX, CY), F32),
                pltpu.VMEM((NZ * CX, NSRC), jnp.bfloat16),
                pltpu.VMEM((2 * NZ, CX, 128), F32),
                pltpu.VMEM((NZ, CX, CY), F32),
                pltpu.VMEM((NZ, CX, CY), F32),
                pltpu.VMEM((n_slots, CX, CY), F32),
                pltpu.VMEM((n_slots, CX, CY), F32),
                pltpu.VMEM((n_slots, CX, CY), F32),
                pltpu.VMEM((n_slots, CX, CY), F32),
                pltpu.VMEM((6, 2 * NZ, CY), F32),
                pltpu.VMEM((6, 2 * NZ, CY), F32),
                pltpu.VMEM((6, CX, 128), F32),
                pltpu.VMEM((6, CX, 128), F32),
                dma((7,)),
                dma((2, n_gx)),
                dma((2, n_gx)),
                dma((6,)),
                dma((6,)),
                dma((6,)),
                dma((6,)),
            ],
            compiler_params=pltpu.CompilerParams(collective_id=0, has_side_effects=True),
        )(idx, source_cells, source_amp, e_field, h_field, target, density)

    return jax.shard_map(
        body,
        mesh=mesh,
        in_specs=placed,
        out_specs=(P(None, None, "gx", "gy"), P(None, None, "gx", "gy"), P("gx", "gy")),
        check_vma=False,
    )
```

time: 538 us -> 83.9 us (0.16); the launches traced: 532 us -> 83.6 us
  local copies, waits for them, and re-layouts: 326 us -> 5.84 us
  waiting for transfers between devices: 75.7 us -> 0 us
  Pallas kernels: 0 us -> 74.3 us
  other arithmetic: 70.6 us -> 2.77 us
  starting transfers between devices: 44.7 us -> 0 us
  between operations: 15.1 us -> 0.7 us
    unnamed x103 -> x8, local copies, waits for them, and re-layouts: 137 us -> 5.76 us
    slice x45 -> x0, local copies, waits for them, and re-layouts: 127 us -> none  [the longest x1 98.1 us: body(): sources_all[timestep]]
    pallas_call x0 -> x1, Pallas kernels: none -> 74.3 us  [body(): pl.pallas_call(run, name='yee_adjoint', out_shape=(jax.ShapeDtypeStruct(f...]
    all_gather x2 -> x0, waiting for transfers between devices: 70.3 us -> none  [collect(): lax.all_gather(design_rows, 'gx', axis=0, tiled=True)]
    scatter-add x1 -> x0, other arithmetic: 48.3 us -> none  [build_sources(): empty.at[:, :, source_cells[0], local_x, local_y]]
    ppermute x12 -> x0, starting transfers between devices: 44.7 us -> none  [shifted(): return lax.ppermute(x, axis, pairs)]
    broadcast_in_dim x1 -> x0, local copies, waits for them, and re-layouts: 32 us -> none  [build_sources(): empty = jnp.zeros((STEPS, 3, NZ, extent_x, extent_y), jnp.float32)]
    another operation x26 -> x1, local copies, waits for them, and re-layouts: 11.3 us -> 0.08 us  [index_tables(): ids = region_list[:, 0].reshape(n_gx, NZ)]
  transfers between devices with their start and end apart: 14 -> 0, of which waited for: 3 -> 0; matrix products, arithmetic and copies ran while one was open for 65% -> 0% of each run, Pallas kernels for 0% -> 0%
where the time goes in v1:
time: 83.9 us; the launch traced here: 83.6 us
  Pallas kernels  74.3 us (89%)
  local copies, waits for them, and re-layouts  5.84 us (7%)
  other arithmetic  2.77 us (3%)
    pallas_call x1, Pallas kernels, body(): pl.pallas_call(run, name='yee_adjoint', out_shape=(jax.ShapeDtypeStruct(f...  74.3 us
    unnamed x8, local copies, waits for them, and re-layouts  5.76 us

profile of v1, /device:TPU:1, one launch (start us, length us, event | category | flops | bytes accessed | tf_op | source)
XLA Modules:
  0.0 83.6 jit_solution(4147708065857450679)
XLA Ops:
  0.7 0.7 reduce
  1.4 0.1 reshape_squeeze.3
  1.5 0.4 convert_reduce_fusion
  1.9 0.1 select_reduce_fusion.2
  2.0 0.1 compare_select_fusion
  2.1 0.6 select_reduce_fusion
  2.7 0.2 select_reduce_fusion.1
  2.9 0.6 pad_add_fusion.refs_0_
  3.5 1.3 %copy.11.refs_2_ = f32[2,3,512]{2,1,0:T(4,128)} copy(f32[2,3,512]{2,0,1:T(2,128)} %param.13) | data formatting | bytes 24576 | tf_op args[6]
  4.8 74.3 %yee_adjoint.1 = (f32[3,24,16,256]{3,2,1,0:T(8,128)}, f32[3,24,16,256]{3,2,1,0:T(8,128)}, f32[24,4096]{1,0:T(8,128)}) custom-call(s32[144]{0:T(256)} %pad_add_fusion.refs_0_, s32[3,512]{1,0:T(4,128)} %refs_1_.1, f32[2,3,512]{2,1,0:T(4,128)} %copy.11.refs_2_, f32[3,24,16,256]{3,2,1,0:T(8,128)} %refs_3_.1, f32[3,24,16,256]{3,2,1,0:T(8,128)} %refs_4_.1, ...), custom_call_target="tpu_custom_call" | custom-call | tf_op jit(solution)/shard_map/yee_adjoint/pallas_call | solution.py:425
  79.1 0.0 copy-start
  79.1 2.5 %copy.15 = f32[3,24,16,256]{3,2,1,0:T(8,128)} copy(f32[3,24,16,256]{3,2,1,0:T(8,128)} %get-tuple-element.9) | data formatting | bytes 2359296
  81.6 0.0 copy-done
  81.6 0.0 copy-start.1
  81.6 1.0 %copy.16 = f32[3,24,16,256]{3,2,1,0:T(8,128)} copy(f32[3,24,16,256]{3,2,1,0:T(8,128)S(1)} %copy-done) | data formatting | bytes 2359296
  82.6 0.2 copy-done.1
  82.8 0.7 copy.17
  (5 shorter events, 0.0 us)
Async XLA Ops:
  79.1 2.5 %copy-start = (f32[3,24,16,256]{3,2,1,0:T(8,128)S(1)}, f32[3,24,16,256]{3,2,1,0:T(8,128)}, u32[]{:S(2)}) copy-start(f32[3,24,16,256]{3,2,1,0:T(8,128)} %get-tuple-element.10) | copy-start | bytes 3538948
  81.6 1.2 %copy-start.1 = (f32[24,4096]{1,0:T(8,128)S(1)}, f32[24,4096]{1,0:T(8,128)}, u32[]{:S(2)}) copy-start(f32[24,4096]{1,0:T(8,128)} %get-tuple-element.11) | copy-start | bytes 1179652

commit v2 on v1

--- a/solution.py
+++ b/solution.py
@@ -109,7 +109,7 @@
             row_lines[pl.ds(half * NZ * CX + a, NZ, stride=CX), :] = projected[:, half * 128:half * 128 + 128]
         return carry
 
-    lax.fori_loop(0, CX, rows_in, 0)
+    lax.fori_loop(0, CX, rows_in, 0, unroll=CX)
 
     def pack_rows(slot, carry):
         row = idx[slot]
@@ -117,7 +117,7 @@
         SEND1[slot, :, 128:256] = ROW[NZ + row]
         return carry
 
-    lax.fori_loop(0, n_slots, pack_rows, 0)
+    lax.fori_loop(0, n_slots, pack_rows, 0, unroll=8)
 
     def pack_low(acc, z, k, fx, fy, fz):
         XS[k, pl.ds(z, 1), :] = fy[0:1, :]
@@ -203,7 +203,7 @@
     def pack_e0(z, acc):
         return pack_low(acc, z, 0, E[0, z], E[1, z], E[2, z])
 
-    YS[0] = lax.fori_loop(0, NZ, pack_e0, blank)
+    YS[0] = lax.fori_loop(0, NZ, pack_e0, blank, unroll=NZ)
 
     pl.semaphore_wait(barrier, n_gx + 1)
     start_rims(0, True)
@@ -233,7 +233,7 @@
         H[2, z + 1] = hz
         return pack_high(acc, z, 1, hx, hy, hz)
 
-    YS[1] = lax.fori_loop(0, NZ, h_first, blank)
+    YS[1] = lax.fori_loop(0, NZ, h_first, blank, unroll=NZ)
     start_rims(1, False)
 
     local_x = cells[1:2, :] - gx * CX
@@ -247,12 +247,12 @@
         L[pl.ds(pl.multiple_of(z * CX, CX), CX), :] = jnp.where(hit, 1.0, 0.0).astype(jnp.bfloat16)
         return carry
 
-    lax.fori_loop(0, NZ, build_hits, 0)
+    lax.fori_loop(0, NZ, build_hits, 0, unroll=NZ)
     hit_y = lax.broadcasted_iota(jnp.int32, (CY, NSRC), 0) == where_y
 
     for n in range(STEPS):
         for c in range(3):
-            row = amp[n, c:c + 1, :]
+            row = amp[c, n:n + 1, :]
             high = row.astype(jnp.bfloat16).astype(F32)
             rest = row - high
             mid = rest.astype(jnp.bfloat16).astype(F32)
@@ -274,7 +274,7 @@
         C1[2, z] = cz
         return carry
 
-    lax.fori_loop(0, NZ, c_first, 0)
+    lax.fori_loop(0, NZ, c_first, 0, unroll=NZ)
 
     for d in range(1, n_gx):
         row_copy(SEND1, RECV1, d, 0).wait()
@@ -289,7 +289,7 @@
             new.append(value)
         return pack_low(acc, z, 2, *new)
 
-    YS[2] = lax.fori_loop(0, NZ, e_first, blank)
+    YS[2] = lax.fori_loop(0, NZ, e_first, blank, unroll=NZ)
     start_rims(2, True)
     finish_rims(2, True)
 
@@ -302,7 +302,7 @@
             new.append(value)
         return pack_high(acc, z, 3, *new)
 
-    YS[3] = lax.fori_loop(0, NZ, h_second, blank)
+    YS[3] = lax.fori_loop(0, NZ, h_second, blank, unroll=NZ)
     start_rims(3, False)
     save_h = pltpu.make_async_copy(H.at[:, 1:NZ + 1], h_out, local_sem.at[4])
     save_h.start()
@@ -327,7 +327,7 @@
         EG[z] = grad
         return pack_low(acc, z, 4, *new)
 
-    YS[4] = lax.fori_loop(0, NZ, e_second, blank)
+    YS[4] = lax.fori_loop(0, NZ, e_second, blank, unroll=NZ)
     start_rims(4, True)
     save_e = pltpu.make_async_copy(E.at[:, 0:NZ], e_out, local_sem.at[5])
     save_e.start()
@@ -342,7 +342,7 @@
             C2[c, z + 1] = curls[c]
         return pack_high(acc, z, 5, *curls)
 
-    YS[5] = lax.fori_loop(0, NZ, adjoint_h, blank)
+    YS[5] = lax.fori_loop(0, NZ, adjoint_h, blank, unroll=NZ)
     start_rims(5, False)
     finish_rims(5, False)
 
@@ -355,13 +355,13 @@
         EG[z] = (-EPS_SPAN * STEP_DT) * (inv * inv) * grad
         return carry
 
-    lax.fori_loop(0, NZ, adjoint_e, 0)
+    lax.fori_loop(0, NZ, adjoint_e, 0, unroll=NZ)
 
     def pack_planes(slot, carry):
         SEND2[slot] = EG[idx[n_slots + slot]]
         return carry
 
-    lax.fori_loop(0, n_slots, pack_planes, 0)
+    lax.fori_loop(0, n_slots, pack_planes, 0, unroll=8)
     for d in range(1, n_gx):
         row_copy(SEND2, RECV2, d, 1).start()
     for s in range(CAP):
@@ -375,7 +375,7 @@
         ROW[NZ + r] = plane[:, 128:256]
         return carry
 
-    lax.fori_loop(0, NZ, unpack, 0)
+    lax.fori_loop(0, NZ, unpack, 0, unroll=NZ)
 
     def scale(a, carry):
         own = SL[:, pl.ds(pl.multiple_of(a * CY, CY), CY)]
@@ -383,13 +383,13 @@
         D[:, pl.ds(pl.multiple_of((a + 1) * CY, CY), CY)] = jnp.concatenate(parts, axis=1) * own
         return carry
 
-    lax.fori_loop(0, CX, scale, 0)
+    lax.fori_loop(0, CX, scale, 0, unroll=CX)
 
     def rows_out(a, carry):
         SL[:, pl.ds(pl.multiple_of(a * CY, CY), CY)] = smooth(D, a)
         return carry
 
-    lax.fori_loop(0, CX, rows_out, 0)
+    lax.fori_loop(0, CX, rows_out, 0, unroll=CX)
     save_g = pltpu.make_async_copy(SL, g_out, local_sem.at[6])
     save_g.start()
     save_h.wait()
@@ -463,7 +463,7 @@
                 dma((6,)),
             ],
             compiler_params=pltpu.CompilerParams(collective_id=0, has_side_effects=True),
-        )(idx, source_cells, source_amp, e_field, h_field, target, density)
+        )(idx, source_cells, jnp.swapaxes(source_amp, 0, 1), e_field, h_field, target, density)
 
     return jax.shard_map(
         body,

time: 83.9 us -> 64.4 us (0.77)
  Pallas kernels: 74.3 us -> 56.2 us
  local copies, waits for them, and re-layouts: 5.84 us -> 4.52 us
    pallas_call x1, Pallas kernels: 74.3 us -> 56.2 us  [body(): pl.pallas_call(run, name='yee_adjoint', out_shape=(jax.ShapeDtypeStruct(f...]
    unnamed x8 -> x7, local copies, waits for them, and re-layouts: 5.76 us -> 4.44 us
where the time goes in v2:
time: 64.4 us; the launch traced here: 64.2 us
  Pallas kernels  56.2 us (87%)
  local copies, waits for them, and re-layouts  4.52 us (7%)
  other arithmetic  2.77 us (4%)
  between operations  0.7 us (1%)
    pallas_call x1, Pallas kernels, body(): pl.pallas_call(run, name='yee_adjoint', out_shape=(jax.ShapeDtypeStruct(f...  56.2 us
    unnamed x7, local copies, waits for them, and re-layouts  4.44 us

profile of v2, /device:TPU:1, one launch (start us, length us, event | category | flops | bytes accessed | tf_op | source)
XLA Modules:
  0.0 64.2 jit_solution(9397602936815236218)
XLA Ops:
  0.7 0.7 %reduce = s32[384]{0:T(512)S(1)} reduce(s32[384,1]{0,1:T(1,128)} %param.11, s32[]{:T(128)} %constant.27.clone.1), dimensions={1}, to_apply=%param.11.reduce_sub_computation | reduce | bytes 3076 | tf_op args[4]
  1.4 0.1 reshape_squeeze.3
  1.5 0.4 convert_reduce_fusion
  1.9 0.1 select_reduce_fusion.2
  2.0 0.1 compare_select_fusion
  2.1 0.6 select_reduce_fusion
  2.7 0.2 select_reduce_fusion.1
  2.9 0.6 %pad_add_fusion.refs_0_ = s32[144]{0:T(256)} fusion(s32[24]{0:T(128)S(1)} %add_bitcast_fusion, s32[24]{0:T(128)S(1)} %select_reduce_fusion, s32[48]{0:T(128)S(1)} %select_reduce_fusion.1, s32[48]{0:T(128)S(1)} %select_reduce_fusion.2), kind=kLoop, calls=%fused_computation.14 | loop fusion | flops 432 | bytes 1152 | tf_op jit(solution)/shard_map/concatenate | solution.py:49
  3.5 56.2 %yee_adjoint.1 = (f32[3,24,16,256]{3,2,1,0:T(8,128)}, f32[3,24,16,256]{3,2,1,0:T(8,128)}, f32[24,4096]{1,0:T(8,128)}) custom-call(s32[144]{0:T(256)} %pad_add_fusion.refs_0_, s32[3,512]{1,0:T(4,128)} %refs_1_.1, f32[3,2,512]{2,1,0:T(2,128)} %bitcast.3, f32[3,24,16,256]{3,2,1,0:T(8,128)} %refs_3_.1, f32[3,24,16,256]{3,2,1,0:T(8,128)} %refs_4_.1, ...), custom_call_target="tpu_custom_call" | custom-call | tf_op jit(solution)/shard_map/yee_adjoint/pallas_call | solution.py:425
  59.7 0.0 copy-start
  59.7 2.5 %copy.13 = f32[3,24,16,256]{3,2,1,0:T(8,128)} copy(f32[3,24,16,256]{3,2,1,0:T(8,128)} %get-tuple-element.9) | data formatting | bytes 2359296
  62.2 0.0 copy-done
  62.2 0.0 copy-start.1
  62.2 1.0 %copy.14 = f32[3,24,16,256]{3,2,1,0:T(8,128)} copy(f32[3,24,16,256]{3,2,1,0:T(8,128)S(1)} %copy-done) | data formatting | bytes 2359296
  63.2 0.2 copy-done.1
  63.4 0.7 %copy.15 = f32[24,4096]{1,0:T(8,128)} copy(f32[24,4096]{1,0:T(8,128)S(1)} %copy-done.1) | data formatting | bytes 786432
  (5 shorter events, 0.0 us)
Async XLA Ops:
  59.7 2.5 %copy-start = (f32[3,24,16,256]{3,2,1,0:T(8,128)S(1)}, f32[3,24,16,256]{3,2,1,0:T(8,128)}, u32[]{:S(2)}) copy-start(f32[3,24,16,256]{3,2,1,0:T(8,128)} %get-tuple-element.10) | copy-start | bytes 3538948
  62.2 1.2 %copy-start.1 = (f32[24,4096]{1,0:T(8,128)S(1)}, f32[24,4096]{1,0:T(8,128)}, u32[]{:S(2)}) copy-start(f32[24,4096]{1,0:T(8,128)} %get-tuple-element.11) | copy-start | bytes 1179652

commit v3 on v2

v3 whole, which is shorter than its diff:
```python
import jax
import jax.numpy as jnp
from jax import lax
from jax.experimental import pallas as pl
from jax.experimental.pallas import tpu as pltpu
from jax.sharding import PartitionSpec as P

CX = 16
CY = 256
NZ = 24
STEPS = 2
CAP = 3
NSRC = 512
WIDTH = CX * CY

STEP_DT = 0.5
SHARPNESS = 4.0
MIDPOINT = 0.5
EPS_LOW = 1.0
EPS_SPAN = 3.0
TANH_MID = 0.9640275800758169

F32 = jnp.float32
MESH = pl.DeviceIdType.MESH


def index_tables(region_list, n_gx):
    me = lax.axis_index("gx")
    ids = region_list[:, 0].reshape(n_gx, NZ)
    tile, plane = ids // NZ, ids % NZ
    place = jnp.arange(NZ, dtype=jnp.int32)
    earlier = place[None, :] < place[:, None]
    rank = jnp.sum(
        ((tile[:, :, None] == tile[:, None, :]) & earlier[None]).astype(jnp.int32), axis=2
    )
    own_tile = lax.dynamic_slice_in_dim(tile, me, 1)[0]
    own_rank = lax.dynamic_slice_in_dim(rank, me, 1)[0]
    own_slot = own_tile * CAP + own_rank
    slots = jnp.arange(n_gx * CAP, dtype=jnp.int32)
    send_rows = jnp.sum(jnp.where(own_slot[None, :] == slots[:, None], place[None, :], 0), axis=1)
    shard_slot = jnp.arange(n_gx, dtype=jnp.int32)[:, None] * CAP + rank
    shard_slot_here = jnp.where(tile == me, shard_slot, -1)
    send_planes = jnp.sum(
        jnp.where(shard_slot_here[None] == slots[:, None, None], plane[None], 0), axis=(1, 2)
    )
    take_planes = jnp.sum(
        jnp.where(ids[None] == (me * NZ + place)[:, None, None], shard_slot[None], 0), axis=(1, 2)
    )
    return jnp.concatenate([send_rows, send_planes, take_planes, own_slot]).astype(jnp.int32)


def kernel(n_gx, n_gy, idx, cells, amp, e_hbm, h_hbm, t_hbm, d_hbm, e_out, h_out, g_out,
           E, H, T, D, SL, C1, G, S, L, ROW, INV, EG, SEND1, RECV1, SEND2, RECV2,
           XL, XLR, XH, XHR, YL, YLR, YH, YHR, XC, YC, HSX,
           local_sem, row_send, row_recv, rim_send, rim_recv):
    gx = lax.axis_index("gx")
    gy = lax.axis_index("gy")
    n_slots = n_gx * CAP
    row_lines = ROW.reshape(2 * NZ * CX, 128)

    def turned(x_by, y_by):
        return (lax.rem(gx + x_by + n_gx, n_gx), lax.rem(gy + y_by + n_gy, n_gy))

    others = [(d, 0) for d in range(1, n_gx)] + [(0, 1), (0, -1), (1, -1), (-1, 1)]
    barrier = pltpu.get_barrier_semaphore()
    for x_by, y_by in others:
        pl.semaphore_signal(barrier, inc=1, device_id=turned(x_by, y_by), device_id_type=MESH)

    load_e = pltpu.make_async_copy(e_hbm, E.at[:, 0:NZ], local_sem.at[1])
    load_h = pltpu.make_async_copy(h_hbm, H, local_sem.at[2])
    load_d = pltpu.make_async_copy(d_hbm, D.at[:, CY:CY + WIDTH], local_sem.at[0])
    load_t = pltpu.make_async_copy(t_hbm, T, local_sem.at[3])
    load_e.start()
    load_h.start()
    load_d.start()
    load_t.start()

    zero_plane = jnp.zeros((CX, CY), F32)
    for c in range(3):
        E[c, NZ] = zero_plane
        G[c, NZ] = zero_plane
    D[:, 0:CY] = jnp.zeros((NZ, CY), F32)
    D[:, CY + WIDTH:] = jnp.zeros((NZ, CY), F32)

    lane_wide = lax.broadcasted_iota(jnp.int32, (NZ, CY), 1)
    sub_wide = lax.broadcasted_iota(jnp.int32, (NZ, CY), 0)
    sub = lax.broadcasted_iota(jnp.int32, (CX, CY), 0)
    sub128 = lax.broadcasted_iota(jnp.int32, (CX, 128), 0)
    lane128 = lax.broadcasted_iota(jnp.int32, (CX, 128), 1)
    lane24 = lax.broadcasted_iota(jnp.int32, (NZ, 128), 1)
    first_row, last_row = sub == 0, sub == CX - 1
    first_lane, last_lane = lane128 == 0, lane128 == 127
    wide_first, wide_last = lane_wide == 0, lane_wide == CY - 1
    blank = jnp.zeros((CX, 128), F32)

    def pack_rims(k, z, acc, field, more=None):
        low, high = acc
        fx, fy, fz = field
        XL[k, z:z + 1, :] = fy[0:1, :]
        XL[k, NZ + z:NZ + z + 1, :] = fz[0:1, :]
        for n, v in enumerate((fx, fz)):
            lane = n * NZ + z
            low = jnp.where(lane128 == lane, pltpu.roll(v[:, 0:128], lane, 1), low)
        flat = [fx, fy, fz]
        tall = [fx, fy, fz]
        if more is not None:
            flat += [more[1], more[2]]
            tall += [more[0], more[2]]
        for n, v in enumerate(flat):
            XH[k, n * NZ + z:n * NZ + z + 1, :] = v[CX - 1:CX, :]
        for n, v in enumerate(tall):
            lane = n * NZ + z
            high = jnp.where(lane128 == lane, pltpu.roll(v[:, 128:256], lane + 1, 1), high)
        return low, high

    def rim_copies(k):
        tall = (5 if k == 0 else 3) * NZ
        moves = [
            (XH.at[k, 0:tall], XHR.at[k, 0:tall], (1, 0)),
            (XL.at[k], XLR.at[k], (-1, 0)),
            (XH.at[k, 0:NZ, 0:128], XC.at[k], (1, -1)),
            (YH.at[k, 0:8], YC.at[k], (-1, 1)),
            (YH.at[k], YHR.at[k], (0, 1)),
            (YL.at[k], YLR.at[k], (0, -1)),
        ]
        return [
            pltpu.make_async_remote_copy(
                src_ref=src, dst_ref=dst, send_sem=rim_send.at[k, n], recv_sem=rim_recv.at[k, n],
                device_id=turned(*by), device_id_type=MESH)
            for n, (src, dst, by) in enumerate(moves)
        ]

    def start_rims(k, acc):
        YL[k], YH[k] = acc
        for copy in rim_copies(k):
            copy.start()

    def keep(inside):
        return jnp.where(inside, 1.0, 0.0)

    has_low_x, has_high_x = keep(gx > 0), keep(gx < n_gx - 1)
    has_low_y, has_high_y = keep(gy > 0), keep(gy < n_gy - 1)

    def finish_rims(k):
        for copy in rim_copies(k):
            copy.wait()
        XLR[k] = XLR[k] * has_high_x

    def strips(k):
        ex, ey, ez = (XHR[k, n * NZ:n * NZ + NZ, :] for n in range(3))
        ey_own, ez_own = XL[k, 0:NZ, :], XL[k, NZ:2 * NZ, :]
        corner = pltpu.roll(XC[k], 127, 1) * has_high_y
        turned_y = pltpu.roll(ex, CY - 1, 1)
        upper = jnp.where(lane24 == 127, corner, turned_y[:, 128:256])
        ahead_y = jnp.concatenate([turned_y[:, 0:128], upper], axis=1) - ex
        ahead_z = jnp.where(sub_wide == NZ - 1, 0.0, pltpu.roll(ex, NZ - 1, 0)) - ex
        flat_y = ahead_z - (ez_own - ez)
        flat_z = (ey_own - ey) - ahead_y

        tall, own = YHR[k], YL[k]
        next_z = jnp.where(lane128 == NZ - 1, 0.0, pltpu.roll(tall, 128 - NZ - 1, 1))
        tall_x = (pltpu.roll(own, 128 - NZ, 1) - pltpu.roll(tall, 128 - 2 * NZ, 1)) - (
            next_z - pltpu.roll(tall, 128 - NZ, 1))
        next_x = jnp.where(sub128 == CX - 1, YC[k, 0:1, :] * has_high_x, pltpu.roll(tall, CX - 1, 0))
        tall_z = (next_x - tall) - (pltpu.roll(own, NZ, 1) - pltpu.roll(tall, NZ, 1))
        return flat_y, flat_z, jnp.where(lane128 < NZ, tall_x, tall_z)

    def curl_ahead(here, above, k, z, lat):
        fx, fy, fz = here
        rim_y = XLR[k, z:z + 1, :]
        rim_z = XLR[k, NZ + z:NZ + z + 1, :]
        lat_x = pltpu.roll(lat, 127 - z, 1)
        lat_z = pltpu.roll(lat, 127 - NZ - z, 1)

        def up_x(v, rim):
            return jnp.where(last_row, rim, pltpu.roll(v, CX - 1, 0))

        def up_y(v, lateral):
            r = pltpu.roll(v, CY - 1, 1)
            return jnp.concatenate([r[:, 0:128], jnp.where(last_lane, lateral, r[:, 128:256])], axis=1)

        return (
            (up_y(fz, lat_z) - fz) - (above[1] - fy),
            (above[0] - fx) - (up_x(fz, rim_z) - fz),
            (up_x(fy, rim_y) - fy) - (up_y(fx, lat_x) - fx),
        )

    def curl_behind(here, below, z, lat):
        fx, fy, fz = here
        rim_y = HSX[z:z + 1, :]
        rim_z = HSX[NZ + z:NZ + z + 1, :]
        lat_x = pltpu.roll(lat, (128 - z) % 128, 1)
        lat_z = pltpu.roll(lat, 128 - NZ - z, 1)

        def dn_x(v, rim):
            return jnp.where(first_row, rim, pltpu.roll(v, 1, 0))

        def dn_y(v, lateral):
            r = pltpu.roll(v, 1, 1)
            return jnp.concatenate([jnp.where(first_lane, lateral, r[:, 0:128]), r[:, 128:256]], axis=1)

        return (
            (fz - dn_y(fz, lat_z)) - (fy - below[1]),
            (fx - below[0]) - (fz - dn_x(fz, rim_z)),
            (fy - dn_x(fy, rim_y)) - (fx - dn_y(fx, lat_x)),
        )

    def plane(ref, z):
        return tuple(ref[c, z] for c in range(3))

    load_e.wait()
    load_h.wait()
    acc = (blank, blank)
    for z in range(NZ):
        acc = pack_rims(0, z, acc, plane(E, z), plane(H, z))
    pl.semaphore_wait(barrier, len(others))
    start_rims(0, acc)

    def smooth(ref, a):
        at = (a + 1) * CY
        mid = ref[:, at:at + CY]
        low = ref[:, at - CY:at]
        high = ref[:, at + CY:at + 2 * CY]
        right = jnp.where(wide_last, 0.0, pltpu.roll(mid, CY - 1, 1))
        left = jnp.where(wide_first, 0.0, pltpu.roll(mid, 1, 1))
        return 0.5 * mid + 0.125 * (high + low + right + left)

    load_d.wait()
    for a in range(CX):
        inner = jnp.tanh(SHARPNESS * (smooth(D, a) - MIDPOINT))
        SL[:, a * CY:a * CY + CY] = SHARPNESS * (1.0 - inner * inner) / (2.0 * TANH_MID)
        projected = (TANH_MID + inner) / (2.0 * TANH_MID)
        for half in range(2):
            row_lines[pl.ds(half * NZ * CX + a, NZ, stride=CX), :] = projected[:, half * 128:half * 128 + 128]

    def pack_rows(slot, carry):
        row = idx[slot]
        SEND1[slot, :, 0:128] = ROW[row]
        SEND1[slot, :, 128:256] = ROW[NZ + row]
        return carry

    lax.fori_loop(0, n_slots, pack_rows, 0, unroll=8)

    def row_copy(send, recv, d, which):
        peer = lax.rem(gx + d, n_gx)
        return pltpu.make_async_remote_copy(
            src_ref=send.at[pl.ds(peer * CAP, CAP)], dst_ref=recv.at[pl.ds(gx * CAP, CAP)],
            send_sem=row_send.at[which, d], recv_sem=row_recv.at[which, d],
            device_id=(peer, gy), device_id_type=MESH)

    for d in range(1, n_gx):
        row_copy(SEND1, RECV1, d, 0).start()
    for s in range(CAP):
        RECV1[gx * CAP + s] = SEND1[gx * CAP + s]

    local_x = cells[1:2, :] - gx * CX
    inside = (local_x >= 0) & (local_x < CX)
    where_zx = jnp.where(inside, cells[0:1, :] * CX + local_x, -1)
    where_y = cells[2:3, :] - gy * CY
    sub_src = lax.broadcasted_iota(jnp.int32, (CX, NSRC), 0)
    for z in range(NZ):
        hit = sub_src == where_zx - z * CX
        L[z * CX:z * CX + CX, :] = jnp.where(hit, 1.0, 0.0).astype(jnp.bfloat16)
    hit_y = lax.broadcasted_iota(jnp.int32, (CY, NSRC), 0) == where_y

    for n in range(STEPS):
        for c in range(3):
            row = amp[c, n:n + 1, :]
            high = row.astype(jnp.bfloat16).astype(F32)
            rest = row - high
            mid = rest.astype(jnp.bfloat16).astype(F32)
            low = rest - mid
            total = None
            for part in (high, mid, low):
                cols = jnp.where(hit_y, part, 0.0).astype(jnp.bfloat16)
                term = lax.dot_general(L[...], cols, (((1,), (1,)), ((), ())),
                                       preferred_element_type=F32)
                total = term if total is None else total + term
            S[n * 3 + c] = total.reshape(NZ, CX, CY)

    finish_rims(0)
    flat_y, flat_z, tall = strips(0)
    HSX[0:NZ, :] = (XHR[0, 3 * NZ:4 * NZ, :] - STEP_DT * flat_y) * has_low_x
    HSX[NZ:2 * NZ, :] = (XHR[0, 4 * NZ:5 * NZ, :] - STEP_DT * flat_z) * has_low_x
    lat_h = (pltpu.roll(YHR[0], 128 - 3 * NZ, 1) - STEP_DT * tall) * has_low_y
    lat_e = YLR[0] * has_high_y
    below = (zero_plane, zero_plane, None)
    for z in range(NZ):
        curls = curl_ahead(plane(E, z), plane(E, z + 1), 0, z, lat_e)
        here = tuple(H[c, z] - STEP_DT * curls[c] for c in range(3))
        for c in range(3):
            H[c, z] = here[c]
        curls = curl_behind(here, below, z, lat_h)
        for c in range(3):
            C1[c, z] = curls[c]
        below = here

    for d in range(1, n_gx):
        row_copy(SEND1, RECV1, d, 0).wait()

    acc = (blank, blank)
    for z in range(NZ):
        inv = 1.0 / (EPS_LOW + EPS_SPAN * RECV1[idx[2 * n_slots + z]])
        INV[z] = inv
        here = tuple(E[c, z] + STEP_DT * inv * C1[c, z] + STEP_DT * S[c, z] for c in range(3))
        for c in range(3):
            E[c, z] = here[c]
        acc = pack_rims(1, z, acc, here)
    start_rims(1, acc)
    load_t.wait()
    finish_rims(1)
    flat_y, flat_z, tall = strips(1)
    HSX[0:NZ, :] = (HSX[0:NZ, :] - STEP_DT * flat_y) * has_low_x
    HSX[NZ:2 * NZ, :] = (HSX[NZ:2 * NZ, :] - STEP_DT * flat_z) * has_low_x
    lat_h = (lat_h - STEP_DT * tall) * has_low_y
    lat_e = YLR[1] * has_high_y

    acc = (blank, blank)
    below = (zero_plane, zero_plane, None)
    for z in range(NZ):
        curls = curl_ahead(plane(E, z), plane(E, z + 1), 1, z, lat_e)
        here = tuple(H[c, z] - STEP_DT * curls[c] for c in range(3))
        for c in range(3):
            H[c, z] = here[c]
        curls = curl_behind(here, below, z, lat_h)
        below = here
        half_inv = STEP_DT * INV[z]
        grad = None
        scaled = []
        for c in range(3):
            value = E[c, z] + half_inv * curls[c] + STEP_DT * S[3 + c, z]
            E[c, z] = value
            misfit = value - T[c, z]
            T[c, z] = misfit
            grad = curls[c] * misfit if grad is None else grad + curls[c] * misfit
            value = half_inv * misfit
            G[c, z] = value
            scaled.append(value)
        EG[z] = grad
        acc = pack_rims(2, z, acc, scaled)
    start_rims(2, acc)
    save_h = pltpu.make_async_copy(H, h_out, local_sem.at[4])
    save_h.start()
    save_e = pltpu.make_async_copy(E.at[:, 0:NZ], e_out, local_sem.at[5])
    save_e.start()
    finish_rims(2)
    flat_y, flat_z, tall = strips(2)
    HSX[0:NZ, :] = flat_y * has_low_x
    HSX[NZ:2 * NZ, :] = flat_z * has_low_x
    lat_h = tall * has_low_y
    lat_e = YLR[2] * has_high_y

    below = (zero_plane, zero_plane, None)
    for z in range(NZ):
        here = curl_ahead(plane(G, z), plane(G, z + 1), 2, z, lat_e)
        curls = curl_behind(here, below, z, lat_h)
        below = here
        grad = EG[z]
        for c in range(3):
            grad = grad + C1[c, z] * (T[c, z] - STEP_DT * curls[c])
        inv = INV[z]
        EG[z] = (-EPS_SPAN * STEP_DT) * (inv * inv) * grad

    def pack_planes(slot, carry):
        SEND2[slot] = EG[idx[n_slots + slot]]
        return carry

    lax.fori_loop(0, n_slots, pack_planes, 0, unroll=8)
    for d in range(1, n_gx):
        row_copy(SEND2, RECV2, d, 1).start()
    for s in range(CAP):
        RECV2[gx * CAP + s] = SEND2[gx * CAP + s]
    for d in range(1, n_gx):
        row_copy(SEND2, RECV2, d, 1).wait()

    for r in range(NZ):
        rows = RECV2[idx[2 * n_slots + NZ + r]]
        ROW[r] = rows[:, 0:128]
        ROW[NZ + r] = rows[:, 128:256]
    for a in range(CX):
        parts = [row_lines[pl.ds(half * NZ * CX + a, NZ, stride=CX), :] for half in range(2)]
        D[:, (a + 1) * CY:(a + 2) * CY] = jnp.concatenate(parts, axis=1) * SL[:, a * CY:a * CY + CY]
    for a in range(CX):
        SL[:, a * CY:a * CY + CY] = smooth(D, a)
    save_g = pltpu.make_async_copy(SL, g_out, local_sem.at[6])
    save_g.start()
    save_h.wait()
    save_e.wait()
    save_g.wait()


def solution(mesh):
    n_gx, n_gy = mesh.shape["gx"], mesh.shape["gy"]
    n_slots = n_gx * CAP
    placed = (
        P(None, None, "gx", "gy"),
        P(None, None, "gx", "gy"),
        P(None, None, "gx", "gy"),
        P("gx", "gy"),
        P(None, "gy"),
        P(),
        P(),
    )
    field = (3, NZ, CX, CY)
    padded = (3, NZ + 1, CX, CY)

    def body(e_field, h_field, target, density, region_list, source_cells, source_amp):
        idx = index_tables(region_list, n_gx)
        any_spec = pl.BlockSpec(memory_space=pl.ANY)
        vmem = pl.BlockSpec(memory_space=pltpu.VMEM)
        smem = pl.BlockSpec(memory_space=pltpu.SMEM)

        def run(*refs):
            kernel(n_gx, n_gy, *refs)

        dma = pltpu.SemaphoreType.DMA
        return pl.pallas_call(
            run,
            name="yee_adjoint",
            out_shape=(
                jax.ShapeDtypeStruct(field, F32),
                jax.ShapeDtypeStruct(field, F32),
                jax.ShapeDtypeStruct((NZ, WIDTH), F32),
            ),
            in_specs=[smem, vmem, vmem, any_spec, any_spec, any_spec, any_spec],
            out_specs=(any_spec, any_spec, any_spec),
            scratch_shapes=[
                pltpu.VMEM(padded, F32),
                pltpu.VMEM(field, F32),
                pltpu.VMEM(field, F32),
                pltpu.VMEM((NZ, WIDTH + 2 * CY), F32),
                pltpu.VMEM((NZ, WIDTH), F32),
                pltpu.VMEM(field, F32),
                pltpu.VMEM(padded, F32),
                pltpu.VMEM((STEPS * 3, NZ, CX, CY), F32),
                pltpu.VMEM((NZ * CX, NSRC), jnp.bfloat16),
                pltpu.VMEM((2 * NZ, CX, 128), F32),
                pltpu.VMEM((NZ, CX, CY), F32),
                pltpu.VMEM((NZ, CX, CY), F32),
                pltpu.VMEM((n_slots, CX, CY), F32),
                pltpu.VMEM((n_slots, CX, CY), F32),
                pltpu.VMEM((n_slots, CX, CY), F32),
                pltpu.VMEM((n_slots, CX, CY), F32),
                pltpu.VMEM((3, 2 * NZ, CY), F32),
                pltpu.VMEM((3, 2 * NZ, CY), F32),
                pltpu.VMEM((3, 5 * NZ, CY), F32),
                pltpu.VMEM((3, 5 * NZ, CY), F32),
                pltpu.VMEM((3, CX, 128), F32),
                pltpu.VMEM((3, CX, 128), F32),
                pltpu.VMEM((3, CX, 128), F32),
                pltpu.VMEM((3, CX, 128), F32),
                pltpu.VMEM((3, NZ, 128), F32),
                pltpu.VMEM((3, 8, 128), F32),
                pltpu.VMEM((2 * NZ, CY), F32),
                dma((7,)),
                dma((2, n_gx)),
                dma((2, n_gx)),
                dma((3, 6)),
                dma((3, 6)),
            ],
            compiler_params=pltpu.CompilerParams(collective_id=0, has_side_effects=True),
        )(idx, source_cells, jnp.swapaxes(source_amp, 0, 1), e_field, h_field, target, density)

    return jax.shard_map(
        body,
        mesh=mesh,
        in_specs=placed,
        out_specs=(P(None, None, "gx", "gy"), P(None, None, "gx", "gy"), P("gx", "gy")),
        check_vma=False,
    )
```

time: 64.4 us -> 60.3 us (0.936)
  Pallas kernels: 56.2 us -> 52 us
    pallas_call x1, Pallas kernels: 56.2 us -> 52 us  [body(): pl.pallas_call(run, name='yee_adjoint', out_shape=(jax.ShapeDtypeStruct(f...]
where the time goes in v3:
time: 60.3 us; the launch traced here: 60 us
  Pallas kernels  52 us (86%)
  local copies, waits for them, and re-layouts  4.52 us (7%)
  other arithmetic  2.77 us (5%)
  between operations  0.7 us (1%)
    pallas_call x1, Pallas kernels, body(): pl.pallas_call(run, name='yee_adjoint', out_shape=(jax.ShapeDtypeStruct(f...  52 us
    unnamed x7, local copies, waits for them, and re-layouts  4.44 us

profile of v3, /device:TPU:1, one launch (start us, length us, event | category | flops | bytes accessed | tf_op | source)
XLA Modules:
  0.0 60.0 jit_solution(16737559803468744860)
XLA Ops:
  0.7 0.7 %reduce = s32[384]{0:T(512)S(1)} reduce(s32[384,1]{0,1:T(1,128)} %param.11, s32[]{:T(128)} %constant.27.clone.1), dimensions={1}, to_apply=%param.11.reduce_sub_computation | reduce | bytes 3076 | tf_op args[4]
  1.4 0.1 reshape_squeeze.3
  1.5 0.4 convert_reduce_fusion
  1.9 0.1 select_reduce_fusion.2
  2.0 0.1 compare_select_fusion
  2.1 0.6 select_reduce_fusion
  2.7 0.2 select_reduce_fusion.1
  2.9 0.6 %pad_add_fusion.refs_0_ = s32[144]{0:T(256)} fusion(s32[24]{0:T(128)S(1)} %add_bitcast_fusion, s32[24]{0:T(128)S(1)} %select_reduce_fusion, s32[48]{0:T(128)S(1)} %select_reduce_fusion.1, s32[48]{0:T(128)S(1)} %select_reduce_fusion.2), kind=kLoop, calls=%fused_computation.14 | loop fusion | flops 432 | bytes 1152 | tf_op jit(solution)/shard_map/concatenate | solution.py:49
  3.5 52.0 %yee_adjoint.1 = (f32[3,24,16,256]{3,2,1,0:T(8,128)}, f32[3,24,16,256]{3,2,1,0:T(8,128)}, f32[24,4096]{1,0:T(8,128)}) custom-call(s32[144]{0:T(256)} %pad_add_fusion.refs_0_, s32[3,512]{1,0:T(4,128)} %refs_1_.1, f32[3,2,512]{2,1,0:T(2,128)} %bitcast.3, f32[3,24,16,256]{3,2,1,0:T(8,128)} %refs_3_.1, f32[3,24,16,256]{3,2,1,0:T(8,128)} %refs_4_.1, ...), custom_call_target="tpu_custom_call" | custom-call | tf_op jit(solution)/shard_map/yee_adjoint/pallas_call | solution.py:417
  55.5 0.0 copy-start
  55.6 2.5 %copy.13 = f32[3,24,16,256]{3,2,1,0:T(8,128)} copy(f32[3,24,16,256]{3,2,1,0:T(8,128)} %get-tuple-element.9) | data formatting | bytes 2359296
  58.0 0.0 copy-done
  58.0 0.0 copy-start.1
  58.0 1.0 %copy.14 = f32[3,24,16,256]{3,2,1,0:T(8,128)} copy(f32[3,24,16,256]{3,2,1,0:T(8,128)S(1)} %copy-done) | data formatting | bytes 2359296
  59.0 0.2 copy-done.1
  59.3 0.7 %copy.15 = f32[24,4096]{1,0:T(8,128)} copy(f32[24,4096]{1,0:T(8,128)S(1)} %copy-done.1) | data formatting | bytes 786432
  (5 shorter events, 0.0 us)
Async XLA Ops:
  55.5 2.5 %copy-start = (f32[3,24,16,256]{3,2,1,0:T(8,128)S(1)}, f32[3,24,16,256]{3,2,1,0:T(8,128)}, u32[]{:S(2)}) copy-start(f32[3,24,16,256]{3,2,1,0:T(8,128)} %get-tuple-element.10) | copy-start | bytes 3538948
  58.0 1.2 %copy-start.1 = (f32[24,4096]{1,0:T(8,128)S(1)}, f32[24,4096]{1,0:T(8,128)}, u32[]{:S(2)}) copy-start(f32[24,4096]{1,0:T(8,128)} %get-tuple-element.11) | copy-start | bytes 1179652

commit v4 on v3

--- a/solution.py
+++ b/solution.py
@@ -24,34 +24,9 @@
 MESH = pl.DeviceIdType.MESH
 
 
-def index_tables(region_list, n_gx):
-    me = lax.axis_index("gx")
-    ids = region_list[:, 0].reshape(n_gx, NZ)
-    tile, plane = ids // NZ, ids % NZ
-    place = jnp.arange(NZ, dtype=jnp.int32)
-    earlier = place[None, :] < place[:, None]
-    rank = jnp.sum(
-        ((tile[:, :, None] == tile[:, None, :]) & earlier[None]).astype(jnp.int32), axis=2
-    )
-    own_tile = lax.dynamic_slice_in_dim(tile, me, 1)[0]
-    own_rank = lax.dynamic_slice_in_dim(rank, me, 1)[0]
-    own_slot = own_tile * CAP + own_rank
-    slots = jnp.arange(n_gx * CAP, dtype=jnp.int32)
-    send_rows = jnp.sum(jnp.where(own_slot[None, :] == slots[:, None], place[None, :], 0), axis=1)
-    shard_slot = jnp.arange(n_gx, dtype=jnp.int32)[:, None] * CAP + rank
-    shard_slot_here = jnp.where(tile == me, shard_slot, -1)
-    send_planes = jnp.sum(
-        jnp.where(shard_slot_here[None] == slots[:, None, None], plane[None], 0), axis=(1, 2)
-    )
-    take_planes = jnp.sum(
-        jnp.where(ids[None] == (me * NZ + place)[:, None, None], shard_slot[None], 0), axis=(1, 2)
-    )
-    return jnp.concatenate([send_rows, send_planes, take_planes, own_slot]).astype(jnp.int32)
-
-
-def kernel(n_gx, n_gy, idx, cells, amp, e_hbm, h_hbm, t_hbm, d_hbm, e_out, h_out, g_out,
+def kernel(n_gx, n_gy, listed, cells, amp, e_hbm, h_hbm, t_hbm, d_hbm, e_out, h_out, g_out,
            E, H, T, D, SL, C1, G, S, L, ROW, INV, EG, SEND1, RECV1, SEND2, RECV2,
-           XL, XLR, XH, XHR, YL, YLR, YH, YHR, XC, YC, HSX,
+           XL, XLR, XH, XHR, YL, YLR, YH, YHR, XC, YC, HSX, TV, idx,
            local_sem, row_send, row_recv, rim_send, rim_recv):
     gx = lax.axis_index("gx")
     gy = lax.axis_index("gy")
@@ -70,10 +45,45 @@
     load_h = pltpu.make_async_copy(h_hbm, H, local_sem.at[2])
     load_d = pltpu.make_async_copy(d_hbm, D.at[:, CY:CY + WIDTH], local_sem.at[0])
     load_t = pltpu.make_async_copy(t_hbm, T, local_sem.at[3])
+    load_d.start()
     load_e.start()
     load_h.start()
-    load_d.start()
     load_t.start()
+
+    n_rows = n_gx * NZ
+    ids = jnp.broadcast_to(listed[...], (8, n_rows))
+    row_at = lax.broadcasted_iota(jnp.int32, (8, n_rows), 1)
+    tile = (ids * 2731) >> 16
+    shard = (row_at * 2731) >> 16
+    place = row_at - shard * NZ
+    rank = jnp.zeros((8, n_rows), jnp.int32)
+    for d in range(1, NZ):
+        same = (pltpu.roll(tile, d, 1) == tile) & (place >= d)
+        rank = rank + jnp.where(same, 1, 0)
+    to_slot = tile * CAP + rank
+    from_slot = shard * CAP + rank
+
+    def hits(values, count):
+        at = lax.broadcasted_iota(jnp.int32, (count, n_rows), 0)
+        return jnp.where(jnp.broadcast_to(values[0:1, :], (count, n_rows)) == at, 1.0, 0.0)
+
+    table = jnp.concatenate([
+        hits(jnp.where(shard == gx, to_slot, -1), n_slots),
+        hits(jnp.where(tile == gx, from_slot, -1), n_slots),
+        hits(ids - gx * NZ, NZ),
+        hits(row_at - gx * NZ, NZ),
+        jnp.zeros((256 - 2 * n_slots - 2 * NZ, n_rows), F32),
+    ], axis=0).astype(jnp.bfloat16)
+    row8 = lax.broadcasted_iota(jnp.int32, (8, n_rows), 0)
+    found = jnp.where(row8 == 0, place, jnp.where(
+        row8 == 1, ids - tile * NZ, jnp.where(row8 == 2, from_slot, to_slot)))
+    entries = lax.dot_general(
+        found.astype(F32).astype(jnp.bfloat16), table, (((1,), (1,)), ((), ())),
+        preferred_element_type=F32).astype(jnp.int32)
+    row256 = lax.broadcasted_iota(jnp.int32, (8, 256), 0)
+    TV[...] = jnp.clip(entries, 0, jnp.where(row256 < 2, NZ - 1, n_slots - 1))
+    load_idx = pltpu.make_async_copy(TV, idx, local_sem.at[7])
+    load_idx.start()
 
     zero_plane = jnp.zeros((CX, CY), F32)
     for c in range(3):
@@ -208,14 +218,6 @@
     def plane(ref, z):
         return tuple(ref[c, z] for c in range(3))
 
-    load_e.wait()
-    load_h.wait()
-    acc = (blank, blank)
-    for z in range(NZ):
-        acc = pack_rims(0, z, acc, plane(E, z), plane(H, z))
-    pl.semaphore_wait(barrier, len(others))
-    start_rims(0, acc)
-
     def smooth(ref, a):
         at = (a + 1) * CY
         mid = ref[:, at:at + CY]
@@ -234,12 +236,21 @@
             row_lines[pl.ds(half * NZ * CX + a, NZ, stride=CX), :] = projected[:, half * 128:half * 128 + 128]
 
     def pack_rows(slot, carry):
-        row = idx[slot]
+        row = jnp.clip(idx[0, slot], 0, NZ - 1)
         SEND1[slot, :, 0:128] = ROW[row]
         SEND1[slot, :, 128:256] = ROW[NZ + row]
         return carry
 
+    load_idx.wait()
     lax.fori_loop(0, n_slots, pack_rows, 0, unroll=8)
+
+    load_e.wait()
+    load_h.wait()
+    acc = (blank, blank)
+    for z in range(NZ):
+        acc = pack_rims(0, z, acc, plane(E, z), plane(H, z))
+    pl.semaphore_wait(barrier, len(others))
+    start_rims(0, acc)
 
     def row_copy(send, recv, d, which):
         peer = lax.rem(gx + d, n_gx)
@@ -300,7 +311,7 @@
 
     acc = (blank, blank)
     for z in range(NZ):
-        inv = 1.0 / (EPS_LOW + EPS_SPAN * RECV1[idx[2 * n_slots + z]])
+        inv = 1.0 / (EPS_LOW + EPS_SPAN * RECV1[jnp.clip(idx[2, 2 * n_slots + z], 0, n_slots - 1)])
         INV[z] = inv
         here = tuple(E[c, z] + STEP_DT * inv * C1[c, z] + STEP_DT * S[c, z] for c in range(3))
         for c in range(3):
@@ -362,7 +373,7 @@
         EG[z] = (-EPS_SPAN * STEP_DT) * (inv * inv) * grad
 
     def pack_planes(slot, carry):
-        SEND2[slot] = EG[idx[n_slots + slot]]
+        SEND2[slot] = EG[jnp.clip(idx[1, n_slots + slot], 0, NZ - 1)]
         return carry
 
     lax.fori_loop(0, n_slots, pack_planes, 0, unroll=8)
@@ -374,7 +385,7 @@
         row_copy(SEND2, RECV2, d, 1).wait()
 
     for r in range(NZ):
-        rows = RECV2[idx[2 * n_slots + NZ + r]]
+        rows = RECV2[jnp.clip(idx[3, 2 * n_slots + NZ + r], 0, n_slots - 1)]
         ROW[r] = rows[:, 0:128]
         ROW[NZ + r] = rows[:, 128:256]
     for a in range(CX):
@@ -405,10 +416,8 @@
     padded = (3, NZ + 1, CX, CY)
 
     def body(e_field, h_field, target, density, region_list, source_cells, source_amp):
-        idx = index_tables(region_list, n_gx)
         any_spec = pl.BlockSpec(memory_space=pl.ANY)
         vmem = pl.BlockSpec(memory_space=pltpu.VMEM)
-        smem = pl.BlockSpec(memory_space=pltpu.SMEM)
 
         def run(*refs):
             kernel(n_gx, n_gy, *refs)
@@ -422,7 +431,7 @@
                 jax.ShapeDtypeStruct(field, F32),
                 jax.ShapeDtypeStruct((NZ, WIDTH), F32),
             ),
-            in_specs=[smem, vmem, vmem, any_spec, any_spec, any_spec, any_spec],
+            in_specs=[vmem, vmem, vmem, any_spec, any_spec, any_spec, any_spec],
             out_specs=(any_spec, any_spec, any_spec),
             scratch_shapes=[
                 pltpu.VMEM(padded, F32),
@@ -452,14 +461,16 @@
                 pltpu.VMEM((3, NZ, 128), F32),
                 pltpu.VMEM((3, 8, 128), F32),
                 pltpu.VMEM((2 * NZ, CY), F32),
-                dma((7,)),
+                pltpu.VMEM((8, 256), jnp.int32),
+                pltpu.SMEM((8, 256), jnp.int32),
+                dma((8,)),
                 dma((2, n_gx)),
                 dma((2, n_gx)),
                 dma((3, 6)),
                 dma((3, 6)),
             ],
             compiler_params=pltpu.CompilerParams(collective_id=0, has_side_effects=True),
-        )(idx, source_cells, jnp.swapaxes(source_amp, 0, 1), e_field, h_field, target, density)
+        )(region_list.T, source_cells, jnp.swapaxes(source_amp, 0, 1), e_field, h_field, target, density)
 
     return jax.shard_map(
         body,

time: 60.3 us -> 57.2 us (0.949)
  other arithmetic: 2.77 us -> 0 us
    reduce_sum x4 -> x0, other arithmetic: 1.31 us -> none  [the longest x1 0.59 us: index_tables(): jnp.sum(jnp.where(ids[None] == (me * NZ + place)[:, None, None], shard_sl...]
    unnamed x1 -> x0, other arithmetic: 0.7 us -> none
    concatenate x1 -> x0, other arithmetic: 0.65 us -> none  [index_tables(): jnp.concatenate([send_rows, send_planes, take_planes, own_slot])]
where the time goes in v4:
time: 57.2 us; the launch traced here: 57 us
  Pallas kernels  51.9 us (91%)
  local copies, waits for them, and re-layouts  4.44 us (8%)
  between operations  0.65 us (1%)
    pallas_call x1, Pallas kernels, body(): pl.pallas_call(run, name='yee_adjoint', out_shape=(jax.ShapeDtypeStruct(f...  51.9 us
    unnamed x7, local copies, waits for them, and re-layouts  4.44 us

profile of v4, /device:TPU:1, one launch (start us, length us, event | category | flops | bytes accessed | tf_op | source)
XLA Modules:
  0.0 57.0 jit_solution(14376915912819067454)
XLA Ops:
  0.6 51.9 %yee_adjoint.1 = (f32[3,24,16,256]{3,2,1,0:T(8,128)}, f32[3,24,16,256]{3,2,1,0:T(8,128)}, f32[24,4096]{1,0:T(8,128)}) custom-call(s32[1,384]{1,0:T(1,128)} %bitcast.3, s32[3,512]{1,0:T(4,128)} %refs_1_.1, f32[3,2,512]{2,1,0:T(2,128)} %bitcast.2, f32[3,24,16,256]{3,2,1,0:T(8,128)} %refs_3_.1, f32[3,24,16,256]{3,2,1,0:T(8,128)} %refs_4_.1, ...), custom_call_target="tpu_custom_call" | custom-call | tf_op jit(solution)/shard_map/yee_adjoint/pallas_call | solution.py:426
  52.5 0.0 copy-start
  52.5 2.5 %copy.13 = f32[3,24,16,256]{3,2,1,0:T(8,128)} copy(f32[3,24,16,256]{3,2,1,0:T(8,128)} %get-tuple-element.6) | data formatting | bytes 2359296
  55.0 0.0 copy-done
  55.0 0.0 copy-start.1
  55.0 1.0 %copy.14 = f32[3,24,16,256]{3,2,1,0:T(8,128)} copy(f32[3,24,16,256]{3,2,1,0:T(8,128)S(1)} %copy-done) | data formatting | bytes 2359296
  56.0 0.2 copy-done.1
  56.2 0.7 %copy.15 = f32[24,4096]{1,0:T(8,128)} copy(f32[24,4096]{1,0:T(8,128)S(1)} %copy-done.1) | data formatting | bytes 786432
Async XLA Ops:
  52.5 2.5 %copy-start = (f32[3,24,16,256]{3,2,1,0:T(8,128)S(1)}, f32[3,24,16,256]{3,2,1,0:T(8,128)}, u32[]{:S(2)}) copy-start(f32[3,24,16,256]{3,2,1,0:T(8,128)} %get-tuple-element.7) | copy-start | bytes 3538948
  55.0 1.2 %copy-start.1 = (f32[24,4096]{1,0:T(8,128)S(1)}, f32[24,4096]{1,0:T(8,128)}, u32[]{:S(2)}) copy-start(f32[24,4096]{1,0:T(8,128)} %get-tuple-element.8) | copy-start | bytes 1179652
